TPU v7x, 256 devices: a whole 4x4x8 slice. The times are simulated.
256 devices in a mesh: row: 16 (over z_hi, x), col: 16 (over y, z_lo, core).
Axes of the slice: x: 4, y: 4, z: 8 (z_hi: 4, z_lo: 2; z = z_hi * 2 + z_lo), core: 2. Of those that a mesh axis runs over, the one named last changes fastest.
Arguments:
- coeffs: bfloat16 [16384, 16384], P('row', 'col'), may hold values from -6 to 6
- alpha_blocks: bfloat16 [128, 2, 5, 128, 128], P('row'), may hold values from -0.25 to 0.25
- alpha_cols: int32 [128, 2, 5], P('row'), may hold values from 0 to 7, as said below
- alpha_list: int32 [16], replicated, may hold values from 0 to 15, as said below
- beta_blocks: bfloat16 [128, 2, 5, 128, 128], P('col'), may hold values from -0.25 to 0.25
- beta_cols: int32 [128, 2, 5], P('col'), may hold values from 0 to 7, as said below
- beta_list: int32 [16], replicated, may hold values from 0 to 15, as said below
Outputs:
- sigma: bfloat16 [16384, 16384], P('row', 'col')
Inputs may be any that keep to these rules, and one draw needn't show every extreme that they name: `alpha_cols`: within each block row and each of its two tile pairs, the 5 block columns are distinct. `beta_cols`: within each block row and each of its two tile pairs, the 5 block columns are distinct. `alpha_list`: entry i is never i. `beta_list`: entry j is never j.
All inputs are finite; a program needn't handle non-finite values.
Results may differ from a plain program's by a relative error of at most 0.001.
Values may be sent and summed in bfloat16 or wider, within the bound.
No kernel may reach another device: no remote copies, remote signals or barrier semaphores. Data moves between devices by JAX's collectives and lax.ppermute only.
A program may use at most 128 MiB of HBM per device.

v0:
```python
import jax
import jax.numpy as jnp
from jax import lax
from jax.experimental import pallas as pl
from jax.experimental.pallas import tpu as pltpu
from jax.sharding import Mesh
from jax.sharding import PartitionSpec as P


def expand(blocks, cols):
    block_count = blocks.shape[0]
    block_size = blocks.shape[3]
    onehot = (cols[..., None] == jnp.arange(block_count, dtype=jnp.int32)).astype(jnp.bfloat16)
    dense_rows = jnp.einsum("rskc,rskij->sricj", onehot, blocks, preferred_element_type=jnp.float32)
    return dense_rows.reshape(2, block_count * block_size, block_count * block_size).astype(
        jnp.bfloat16
    )


def right_product(left, dense_block):
    return lax.dot_general(
        left, dense_block, (((1,), (1,)), ((), ())), preferred_element_type=jnp.float32
    )


def copy_pieces(pools, table, count, codes):
    piece = pools[0].shape[1:]

    def kernel(table_ref, *refs):
        sources = refs[: len(pools)]
        outs = refs[len(pools) : len(pools) + count]
        held, in_sem, out_sem = refs[len(pools) + count :]
        for i, (pool, index) in enumerate(codes(table_ref)):
            for c, source in enumerate(sources):

                @pl.when(pool == c)
                def _():
                    pltpu.make_async_copy(
                        source.at[jnp.minimum(index, source.shape[0] - 1)], held.at[i], in_sem.at[i]
                    ).start()

        for i in range(count):
            pltpu.make_async_copy(sources[0].at[0], held.at[i], in_sem.at[i]).wait()
            pltpu.make_async_copy(held.at[i], outs[i], out_sem.at[i]).start()
        for i in range(count):
            pltpu.make_async_copy(held.at[i], outs[i], out_sem.at[i]).wait()

    return pl.pallas_call(
        kernel,
        out_shape=[jax.ShapeDtypeStruct(piece, pools[0].dtype)] * count,
        grid_spec=pltpu.PrefetchScalarGridSpec(
            num_scalar_prefetch=1,
            grid=(1,),
            in_specs=[pl.BlockSpec(memory_space=pl.ANY)] * len(pools),
            out_specs=[pl.BlockSpec(memory_space=pl.ANY)] * count,
            scratch_shapes=[
                pltpu.VMEM((count,) + piece, pools[0].dtype),
                pltpu.SemaphoreType.DMA((count,)),
                pltpu.SemaphoreType.DMA((count,)),
            ],
        ),
        cost_estimate=pl.CostEstimate(
            flops=0, transcendentals=0, bytes_accessed=4 * count * piece[0] * piece[1]
        ),
    )(table, *pools)


def gather_pieces(pool, table):
    count = table.shape[0]

    def kernel(table_ref, source, out, held, in_sem, out_sem):
        for i in range(count):
            pltpu.make_async_copy(source.at[table_ref[i]], held.at[i], in_sem.at[i]).start()
        for i in range(count):
            pltpu.make_async_copy(source.at[0], held.at[i], in_sem.at[i]).wait()
            pltpu.make_async_copy(held.at[i], out.at[i], out_sem.at[i]).start()
        for i in range(count):
            pltpu.make_async_copy(held.at[i], out.at[i], out_sem.at[i]).wait()

    return pl.pallas_call(
        kernel,
        out_shape=jax.ShapeDtypeStruct(pool.shape, pool.dtype),
        grid_spec=pltpu.PrefetchScalarGridSpec(
            num_scalar_prefetch=1,
            grid=(1,),
            in_specs=[pl.BlockSpec(memory_space=pl.ANY)],
            out_specs=pl.BlockSpec(memory_space=pl.ANY),
            scratch_shapes=[
                pltpu.VMEM(pool.shape, pool.dtype),
                pltpu.SemaphoreType.DMA((count,)),
                pltpu.SemaphoreType.DMA((count,)),
            ],
        ),
        cost_estimate=pl.CostEstimate(flops=0, transcendentals=0, bytes_accessed=4 * pool.size),
    )(table, pool)


def place():
    return lax.axis_index("y"), lax.axis_index("zl"), lax.axis_index("core")


def crossing(table, source, target):
    present = []
    for k in range(8):
        tile = 4 * (k // 2) + 2 * source + k % 2
        hit = jnp.int32(0)
        for d in range(8):
            hit = hit | (table[4 * (d // 2) + 2 * target + d % 2] == tile).astype(jnp.int32)
        present.append(hit)
    return present


def slot_codes(first):
    def codes(table):
        y, z_lo, core = place()
        found = [(jnp.int32(0), jnp.int32(0))] * 2
        rank = jnp.int32(0)
        for k, hit in enumerate(crossing(table, z_lo, 1 - z_lo)):
            pool, index = (core != k % 2).astype(jnp.int32), (y - k // 2 + 4) % 4
            for j in range(2):
                here = (hit == 1) & (rank == 2 * (first + j) + core)
                found[j] = jnp.where(here, pool, found[j][0]), jnp.where(here, index, found[j][1])
            rank = rank + hit
        return found

    return codes


def send_codes(table):
    y, z_lo, core = place()
    present = crossing(table, 1 - z_lo, z_lo)
    found = []
    for t in range(4):
        wanted = table[4 * ((y + t) % 4) + 2 * z_lo + core]
        tile_y, tile_z, tile_core = wanted // 4, (wanted // 2) % 2, wanted % 2
        rank = jnp.int32(0)
        for k in range(8):
            rank = rank + jnp.where(k < 2 * tile_y + tile_core, present[k], 0)
        slot = rank // 2
        near = tile_z == z_lo
        other = jnp.where(near, tile_core, rank % 2) != core
        pool = jnp.where(near, 0, 2 + 2 * slot) + other.astype(jnp.int32)
        found.append((pool, jnp.where(near, (y - tile_y + 4) % 4, 0)))
    return found


def order_codes(table):
    y, z_lo, core = place()
    mine = table[4 * y + 2 * z_lo + core] // 4
    return [((y - mine - i + 8) % 4, jnp.int32(0)) for i in range(4)]


def swap(value, axis):
    return lax.ppermute(value, axis, [(0, 1), (1, 0)])


def exchange(value, axis):
    return lax.all_to_all(value, axis, split_axis=0, concat_axis=0, tiled=True)


def shift(value, axis, step):
    count = lax.axis_size(axis)
    return lax.ppermute(value, axis, [(i, (i + step) % count) for i in range(count)])


def sigma(coeffs, alpha_blocks, alpha_cols, alpha_list, beta_blocks, beta_cols, beta_list):
    strings = coeffs.shape[0]
    rows = 16
    alpha_pieces = coeffs.reshape(rows, strings // rows, strings)
    beta_pieces = coeffs.reshape(4, strings // 4, strings)

    near = [shift(beta_pieces[s], "y", s) for s in (1, 2, 3)]
    near = jnp.stack([beta_pieces[0]] + near)
    alpha_held = exchange(alpha_pieces, ("zh", "x"))

    near_twin = swap(near, "core")
    slots = copy_pieces([near, near_twin], beta_list, 2, slot_codes(0))
    slots = [swap(slot, "zl")[None] for slot in slots]
    slots = [[slot, swap(slot, "core")] for slot in slots]

    counts = [sum(crossing(beta_list, side, 1 - side)) for side in (0, 1)]

    def carry():
        more = copy_pieces([near, near_twin], beta_list, 2, slot_codes(2))
        more = [swap(slot, "zl")[None] for slot in more]
        return [[slot, swap(slot, "core")] for slot in more]

    def skip():
        return slots

    more = lax.cond(jnp.maximum(counts[0], counts[1]) > 4, carry, skip)
    pools = [near, near_twin] + slots[0] + slots[1] + more[0] + more[1]
    leaving = [piece[None] for piece in copy_pieces(pools, beta_list, 4, send_codes)]
    arrived = leaving[:1] + [shift(leaving[s], "y", s) for s in (1, 2, 3)]
    beta_fetched = copy_pieces(arrived, beta_list, 4, order_codes)

    alpha_out = gather_pieces(alpha_held, alpha_list)
    alpha_fetched = exchange(alpha_out, ("zh", "x")).reshape(strings, strings)

    alpha_dense = expand(alpha_blocks, alpha_cols)
    beta_dense = expand(beta_blocks, beta_cols)
    terms = jnp.dot(alpha_dense[0], coeffs, preferred_element_type=jnp.float32)
    terms = terms + right_product(coeffs, beta_dense[0])
    terms = lax.optimization_barrier(terms)
    terms = terms + right_product(jnp.concatenate(beta_fetched), beta_dense[1])
    terms = lax.optimization_barrier(terms)
    terms = terms + jnp.dot(alpha_dense[1], alpha_fetched, preferred_element_type=jnp.float32)
    return terms.astype(jnp.bfloat16)


def solution(mesh):
    fine = Mesh(mesh.devices.reshape(4, 4, 4, 2, 2), ("zh", "x", "y", "zl", "core"))
    row = ("zh", "x")
    col = ("y", "zl", "core")
    placed = (
        P(row, col),
        P(row, None, None, None, None),
        P(row, None, None),
        P(),
        P(col, None, None, None, None),
        P(col, None, None),
        P(),
    )
    return jax.shard_map(sigma, mesh=fine, in_specs=placed, out_specs=P(row, col), check_vma=False)
```

profile of v0, /device:TPU:32, one launch (start us, length us, event | category | flops | bytes accessed | tf_op | source)
XLA Modules:
  0.0 232.2 jit_solution(6554897080192488851)
XLA Ops:
  0.0 10.4 %all-to-all-start = ((bf16[16,64,1024]{2,1,0:T(8,128)(2,1)}), bf16[16,64,1024]{2,1,0:T(8,128)(2,1)}, u32[]{:S(2)}, u32[]{:S(2)}) async-start(bf16[16,64,1024]{2,1,0:T(8,128)(2,1)} %bitcast.60), calls=%async_computation | async-start | bytes 4194304 | tf_op jit(solution)/shard_map/all_to_all | solution.py:158
  12.2 3.3 %collective-permute-start.5 = (bf16[256,1024]{1,0:T(8,128)(2,1)S(1)}, bf16[256,1024]{1,0:T(8,128)(2,1)S(1)}, u32[]{:S(2)}, u32[]{:S(2)}) collective-permute-start(bf16[256,1024]{1,0:T(8,128)(2,1)S(1)} %get-tuple-element.57), channel_id=1, source_target_pairs={{0,8},{4,12},{8,0},{12,4},{1,9},{5,13},{9,1},{13,5},{2,10},{6,14},... | collective-permute-start | bytes 1572872 | tf_op jit(solution)/shard_map/ppermute | solution.py:163
  16.1 2.6 %collective-permute-start.6 = (bf16[256,1024]{1,0:T(8,128)(2,1)S(1)}, bf16[256,1024]{1,0:T(8,128)(2,1)S(1)}, u32[]{:S(2)}, u32[]{:S(2)}) collective-permute-start(bf16[256,1024]{1,0:T(8,128)(2,1)S(1)} %get-tuple-element.59), channel_id=1, source_target_pairs={{0,12},{4,0},{8,4},{12,8},{1,13},{5,1},{9,5},{13,9},{2,14},{6,2},{... | collective-permute-start | bytes 1572872 | tf_op jit(solution)/shard_map/ppermute | solution.py:163
  18.7 9.9 %collective-permute-done.5 = bf16[256,1024]{1,0:T(8,128)(2,1)S(1)} collective-permute-done((bf16[256,1024]{1,0:T(8,128)(2,1)S(1)}, bf16[256,1024]{1,0:T(8,128)(2,1)S(1)}, u32[]{:S(2)}, u32[]{:S(2)}) %collective-permute-start.5) | collective-permute-done | bytes 524320 | tf_op jit(solution)/shard_map/ppermute | solution.py:163
  28.6 9.8 %collective-permute-done.4 = bf16[256,1024]{1,0:T(8,128)(2,1)S(1)} collective-permute-done((bf16[256,1024]{1,0:T(8,128)(2,1)S(1)}, bf16[256,1024]{1,0:T(8,128)(2,1)S(1)}, u32[]{:S(2)}, u32[]{:S(2)}) %collective-permute-start.4) | collective-permute-done | bytes 524320 | tf_op jit(solution)/shard_map/ppermute | solution.py:163
  40.4 21.8 %all-to-all-done.source = bf16[16,64,1024]{2,1,0:T(8,128)(2,1)} async-done(((bf16[16,64,1024]{2,1,0:T(8,128)(2,1)}), bf16[16,64,1024]{2,1,0:T(8,128)(2,1)}, u32[]{:S(2)}, u32[]{:S(2)}) %all-to-all-start) | async-done | bytes 2097184 | tf_op jit(solution)/shard_map/all_to_all | solution.py:158
  62.2 4.4 %shard_map.76 = bf16[16,64,1024]{2,1,0:T(8,128)(2,1)} custom-call(s32[16]{0:T(128)} %table_ref.7, bf16[16,64,1024]{2,1,0:T(8,128)(2,1)} %all-to-all-done.source), custom_call_target="tpu_custom_call" | custom-call | bytes 4194304 | tf_op jit(solution)/shard_map/pallas_call | solution.py:80
  66.7 4.5 %all-to-all-start.1 = ((bf16[16,64,1024]{2,1,0:T(8,128)(2,1)}), bf16[16,64,1024]{2,1,0:T(8,128)(2,1)}, u32[]{:S(2)}, u32[]{:S(2)}) async-start(bf16[16,64,1024]{2,1,0:T(8,128)(2,1)} %shard_map.76), calls=%async_computation.1 | async-start | bytes 4194304 | tf_op jit(solution)/shard_map/all_to_all | solution.py:158
  71.4 3.8 %convert_bitcast_fusion = bf16[2,8,128,8,128]{4,3,2,1,0:T(8,128)(2,1)} fusion(bf16[8,2,5,128,128]{4,3,2,1,0:T(8,128)(2,1)S(1)} %copy-done, s32[8,2,5]{2,0,1:T(8,128)S(1)} %copy.10), kind=kOutput, calls=%fused_computation.6 | convolution fusion | flops 23069312 | bytes 6816064 | tf_op jit(solution)/shard_map/rskc,rskij->sricj/dot_general | solution.py:14
  75.1 3.7 %convert_bitcast_fusion.1 = bf16[2,8,128,8,128]{4,3,2,1,0:T(8,128)(2,1)} fusion(bf16[8,2,5,128,128]{4,3,2,1,0:T(8,128)(2,1)S(1)} %copy-done.3, s32[8,2,5]{2,0,1:T(8,128)S(1)} %copy.8), kind=kOutput, calls=%fused_computation.7 | convolution fusion | flops 23069312 | bytes 6816064 | tf_op jit(solution)/shard_map/rskc,rskij->sricj/dot_general | solution.py:14
  78.8 2.7 %shard_map.73 = (bf16[256,1024]{1,0:T(8,128)(2,1)}, bf16[256,1024]{1,0:T(8,128)(2,1)}) custom-call(s32[16]{0:T(128)S(1)} %copy-done.8, bf16[4,256,1024]{2,1,0:T(8,128)(2,1)} %pad_maximum_fusion.refs_0_, bf16[4,256,1024]{2,1,0:T(8,128)(2,1)} %collective-permute-done.7.refs_1_), custom_call_target="tpu_custom_call" | custom-call | bytes 2097152 | tf_op jit(solution)/shard_map/pallas_call | solution.py:48
  83.7 4.6 %fusion.39 = (bf16[1,8,128,8,128]{4,3,2,1,0:T(8,128)(2,1)}, bf16[1,8,128,8,128]{4,3,2,1,0:T(8,128)(2,1)}) fusion(bf16[2,8,128,8,128]{4,3,2,1,0:T(8,128)(2,1)} %convert_bitcast_fusion), kind=kLoop, calls=%fused_computation.37 | loop fusion | bytes 8388608 | tf_op jit(solution)/shard_map/slice | solution.py:205
  168.8 4.0 %fusion.38 = (bf16[1,8,128,8,128]{4,3,2,1,0:T(8,128)(2,1)}, bf16[1,8,128,8,128]{4,3,2,1,0:T(8,128)(2,1)S(1)}) fusion(bf16[2,8,128,8,128]{4,3,2,1,0:T(8,128)(2,1)} %convert_bitcast_fusion.1), kind=kLoop, calls=%fused_computation.36 | loop fusion | bytes 8388608 | tf_op jit(solution)/shard_map/slice | solution.py:207
  173.4 4.3 %fusion.16 = f32[1024,1024]{1,0:T(8,128)} fusion(bf16[1024,1024]{1,0:T(8,128)(2,1)S(1)} %copy-done.2, bf16[128,8,8,128]{3,2,1,0:T(8,128)(2,1)S(1)} %bitcast.70), kind=kOutput, calls=%fused_computation.16 | convolution fusion | flops 2147483648 | bytes 8388608 | tf_op jit(solution)/shard_map/dot_general | solution.py:202
  177.7 5.5 %conditional.1 = (bf16[1,256,1024]{2,1,0:T(8,128)(2,1)}, bf16[1,256,1024]{2,1,0:T(8,128)(2,1)}, bf16[1,256,1024]{2,1,0:T(8,128)(2,1)}, bf16[1,256,1024]{2,1,0:T(8,128)(2,1)}) conditional(s32[]{:T(128)} %convert_element_type.906, (bf16[1,256,1024]{2,1,0:T(8,128)(2,1)S(1)}, bf16[1,256,1024]{2,1,0:T(8,128)(2,1)}, bf16[1,256,1024]{2,1,0:T(8,128)(2,1)S(1)}, ...), branch_computations={%region_0.0_spmd, %region_1.0_spmd} | conditional | bytes 10485952 | solution.py:191
  183.1 3.6 %shard_map.74 = (bf16[256,1024]{1,0:T(8,128)(2,1)}, bf16[256,1024]{1,0:T(8,128)(2,1)}, bf16[256,1024]{1,0:T(8,128)(2,1)}, bf16[256,1024]{1,0:T(8,128)(2,1)}) custom-call(s32[16]{0:T(128)S(1)} %copy-done.8, bf16[4,256,1024]{2,1,0:T(8,128)(2,1)} %pad_maximum_fusion.refs_0_, bf16[4,256,1024]{2,1,0:T(8,128)(2,1)} %collective-permute-done.7.refs_1_, ...), custom_call_target="tpu_custom_call" | custom-call | bytes 4194304 | tf_op jit(solution)/shard_map/pallas_call | solution.py:48
  188.4 2.9 %collective-permute-start.13 = (bf16[1,256,1024]{2,1,0:T(8,128)(2,1)}, bf16[1,256,1024]{2,1,0:T(8,128)(2,1)S(1)}, u32[]{:S(2)}, u32[]{:S(2)}) collective-permute-start(bf16[1,256,1024]{2,1,0:T(8,128)(2,1)} %bitcast.76), channel_id=1, source_target_pairs={{0,8},{4,12},{8,0},{12,4},{1,9},{5,13},{9,1},{13,5},{2,10},{6,14},... | collective-permute-start | bytes 1572872 | tf_op jit(solution)/shard_map/ppermute | solution.py:163
  192.7 7.2 %bitcast_add_fusion = f32[1024,1024]{1,0:T(8,128)} fusion(f32[1024,1024]{1,0:T(8,128)} %fusion.16, bf16[1024,1024]{1,0:T(8,128)(2,1)S(1)} %copy-done.2, bf16[128,8,8,128]{3,2,1,0:T(8,128)(2,1)} %bitcast.68), kind=kOutput, calls=%fused_computation | convolution fusion | flops 2148532224 | bytes 12582912 | tf_op jit(solution)/shard_map/dot_general | solution.py:21
  199.9 2.1 collective-permute-done.12.refs_1_
  202.0 12.4 %collective-permute-done.13.refs_2_ = bf16[1,256,1024]{2,1,0:T(8,128)(2,1)S(1)} collective-permute-done((bf16[1,256,1024]{2,1,0:T(8,128)(2,1)}, bf16[1,256,1024]{2,1,0:T(8,128)(2,1)S(1)}, u32[]{:S(2)}, u32[]{:S(2)}) %collective-permute-start.13) | collective-permute-done | bytes 524320 | tf_op jit(solution)/shard_map/ppermute | solution.py:163
  215.2 3.0 %shard_map.75 = (bf16[256,1024]{1,0:T(8,128)(2,1)}, bf16[256,1024]{1,0:T(8,128)(2,1)}, bf16[256,1024]{1,0:T(8,128)(2,1)}, bf16[256,1024]{1,0:T(8,128)(2,1)}) custom-call(s32[16]{0:T(128)S(1)} %copy-done.8, bf16[1,256,1024]{2,1,0:T(8,128)(2,1)} %bitcast.71, bf16[1,256,1024]{2,1,0:T(8,128)(2,1)} %copy-done.6, bf16[1,256,1024]{2,1,0:T(8,128)(2,1)} %copy-done.7, ...), custom_call_target="tpu_custom_call" | custom-call | bytes 4194304 | tf_op jit(solution)/shard_map/pallas_call | solution.py:48
  218.2 7.2 %fusion.26 = f32[1024,1024]{1,0:T(8,128)} fusion(f32[1024,1024]{1,0:T(8,128)} %bitcast_add_fusion, bf16[128,8,8,128]{3,2,1,0:T(8,128)(2,1)S(1)} %bitcast.67, bf16[256,1024]{1,0:T(8,128)(2,1)} %get-tuple-element.51, bf16[256,1024]{1,0:T(8,128)(2,1)} %get-tuple-element.50, bf16[256,1024]{1,0:T(8,128)(2,1)} %get-tuple-element.49, ...), kind=kOutput, calls=%fused_computation.27 | convolution fusion | flops 2156920832 | bytes 12582912 | tf_op jit(solution)/shard_map/dot_general | solution.py:21
  225.4 4.7 %fusion.8 = f32[1024,1024]{1,0:T(8,128)S(1)} fusion(bf16[1024,1024]{1,0:T(8,128)(2,1)} %bitcast.24, bf16[128,8,8,128]{3,2,1,0:T(8,128)(2,1)} %bitcast.69), kind=kOutput, calls=%fused_computation.8 | convolution fusion | flops 2147483648 | bytes 8388608 | tf_op jit(solution)/shard_map/dot_general | solution.py:207
  230.1 2.1 add_convert_fusion
  (47 shorter events, 17.3 us)
Async XLA Ops:
  0.0 71.4 %copy-start = (bf16[8,2,5,128,128]{4,3,2,1,0:T(8,128)(2,1)S(1)}, bf16[8,2,5,128,128]{4,3,2,1,0:T(8,128)(2,1)}, u32[]{:S(2)}) copy-start(bf16[8,2,5,128,128]{4,3,2,1,0:T(8,128)(2,1)} %param.13) | copy-start | bytes 7864324
  0.0 62.2 %all-to-all-start = ((bf16[16,64,1024]{2,1,0:T(8,128)(2,1)}), bf16[16,64,1024]{2,1,0:T(8,128)(2,1)}, u32[]{:S(2)}, u32[]{:S(2)}) async-start(bf16[16,64,1024]{2,1,0:T(8,128)(2,1)} %bitcast.60), calls=%async_computation | async-start | bytes 4194304 | tf_op jit(solution)/shard_map/all_to_all | solution.py:158
  12.2 16.4 %collective-permute-start.5 = (bf16[256,1024]{1,0:T(8,128)(2,1)S(1)}, bf16[256,1024]{1,0:T(8,128)(2,1)S(1)}, u32[]{:S(2)}, u32[]{:S(2)}) collective-permute-start(bf16[256,1024]{1,0:T(8,128)(2,1)S(1)} %get-tuple-element.57), channel_id=1, source_target_pairs={{0,8},{4,12},{8,0},{12,4},{1,9},{5,13},{9,1},{13,5},{2,10},{6,14},... | collective-permute-start | bytes 1572872 | tf_op jit(solution)/shard_map/ppermute | solution.py:163
  15.4 22.9 %collective-permute-start.4 = (bf16[256,1024]{1,0:T(8,128)(2,1)S(1)}, bf16[256,1024]{1,0:T(8,128)(2,1)S(1)}, u32[]{:S(2)}, u32[]{:S(2)}) collective-permute-start(bf16[256,1024]{1,0:T(8,128)(2,1)S(1)} %get-tuple-element.58), channel_id=1, source_target_pairs={{0,4},{4,8},{8,12},{12,0},{1,5},{5,9},{9,13},{13,1},{2,6},{6,10},{... | collective-permute-start | bytes 1572872 | tf_op jit(solution)/shard_map/ppermute | solution.py:163
  16.1 22.6 %collective-permute-start.6 = (bf16[256,1024]{1,0:T(8,128)(2,1)S(1)}, bf16[256,1024]{1,0:T(8,128)(2,1)S(1)}, u32[]{:S(2)}, u32[]{:S(2)}) collective-permute-start(bf16[256,1024]{1,0:T(8,128)(2,1)S(1)} %get-tuple-element.59), channel_id=1, source_target_pairs={{0,12},{4,0},{8,4},{12,8},{1,13},{5,1},{9,5},{13,9},{2,14},{6,2},{... | collective-permute-start | bytes 1572872 | tf_op jit(solution)/shard_map/ppermute | solution.py:163
  40.4 38.4 %collective-permute-start.7 = (bf16[4,256,1024]{2,1,0:T(8,128)(2,1)}, bf16[4,256,1024]{2,1,0:T(8,128)(2,1)}, u32[]{:S(2)}, u32[]{:S(2)}) collective-permute-start(bf16[4,256,1024]{2,1,0:T(8,128)(2,1)} %pad_maximum_fusion.refs_0_), channel_id=1, source_target_pairs={{0,1},{1,0},{2,3},{3,2},{4,5},{5,4},{6,7},{7,6},{8,9},{9,8},{10,11... | collective-permute-start | bytes 6291464 | tf_op jit(solution)/shard_map/ppermute | solution.py:154
  66.7 4.5 %copy-start.9 = (s32[8,2,5]{0,1,2:T(2,128)S(1)}, s32[8,2,5]{0,1,2:T(2,128)}, u32[]{:S(2)}) copy-start(s32[8,2,5]{0,1,2:T(2,128)} %param.11) | copy-start | bytes 964
  66.7 4.6 %copy-start.10 = (s32[8,2,5]{0,1,2:T(2,128)S(1)}, s32[8,2,5]{0,1,2:T(2,128)}, u32[]{:S(2)}) copy-start(s32[8,2,5]{0,1,2:T(2,128)} %param.14) | copy-start | bytes 964
  66.7 158.7 %all-to-all-start.1 = ((bf16[16,64,1024]{2,1,0:T(8,128)(2,1)}), bf16[16,64,1024]{2,1,0:T(8,128)(2,1)}, u32[]{:S(2)}, u32[]{:S(2)}) async-start(bf16[16,64,1024]{2,1,0:T(8,128)(2,1)} %shard_map.76), calls=%async_computation.1 | async-start | bytes 4194304 | tf_op jit(solution)/shard_map/all_to_all | solution.py:158
  71.4 3.8 %copy-start.3 = (bf16[8,2,5,128,128]{4,3,2,1,0:T(8,128)(2,1)S(1)}, bf16[8,2,5,128,128]{4,3,2,1,0:T(8,128)(2,1)}, u32[]{:S(2)}) copy-start(bf16[8,2,5,128,128]{4,3,2,1,0:T(8,128)(2,1)} %param.10) | copy-start | bytes 7864324
  75.1 3.7 %copy-start.8 = (s32[16]{0:T(128)S(1)}, s32[16]{0:T(128)}, u32[]{:S(2)}) copy-start(s32[16]{0:T(128)} %table_ref.6) | copy-start | bytes 196
  81.6 91.3 %collective-permute-start.8 = (bf16[256,1024]{1,0:T(8,128)(2,1)}, bf16[256,1024]{1,0:T(8,128)(2,1)S(1)}, u32[]{:S(2)}, u32[]{:S(2)}) collective-permute-start(bf16[256,1024]{1,0:T(8,128)(2,1)} %get-tuple-element.38), channel_id=1, source_target_pairs={{0,2},{2,0},{1,3},{3,1},{4,6},{6,4},{5,7},{7,5},{8,10},{10,8},{9,1... | collective-permute-start | bytes 1572872 | tf_op jit(solution)/shard_map/ppermute | solution.py:154
  82.6 90.2 %collective-permute-start.10 = (bf16[256,1024]{1,0:T(8,128)(2,1)}, bf16[256,1024]{1,0:T(8,128)(2,1)S(1)}, u32[]{:S(2)}, u32[]{:S(2)}) collective-permute-start(bf16[256,1024]{1,0:T(8,128)(2,1)} %get-tuple-element.39), channel_id=1, source_target_pairs={{0,2},{2,0},{1,3},{3,1},{4,6},{6,4},{5,7},{7,5},{8,10},{10,8},{9,1... | collective-permute-start | bytes 1572872 | tf_op jit(solution)/shard_map/ppermute | solution.py:154
  168.8 4.6 %copy-start.2 = (bf16[1024,1024]{1,0:T(8,128)(2,1)S(1)}, bf16[1024,1024]{1,0:T(8,128)(2,1)}, u32[]{:S(2)}) copy-start(bf16[1024,1024]{1,0:T(8,128)(2,1)} %param.9) | copy-start | bytes 6291460
  172.8 4.8 %collective-permute-start.9 = (bf16[1,256,1024]{2,1,0:T(8,128)(2,1)S(1)}, bf16[1,256,1024]{2,1,0:T(8,128)(2,1)}, u32[]{:S(2)}, u32[]{:S(2)}) collective-permute-start(bf16[1,256,1024]{2,1,0:T(8,128)(2,1)S(1)} %bitcast.61), channel_id=1, source_target_pairs={{0,1},{1,0},{2,3},{3,2},{4,5},{5,4},{6,7},{7,6},{8,9},{9,8},{10,11... | collective-permute-start | bytes 1572872 | tf_op jit(solution)/shard_map/ppermute | solution.py:154
  172.8 4.8 %collective-permute-start.11 = (bf16[1,256,1024]{2,1,0:T(8,128)(2,1)S(1)}, bf16[1,256,1024]{2,1,0:T(8,128)(2,1)}, u32[]{:S(2)}, u32[]{:S(2)}) collective-permute-start(bf16[1,256,1024]{2,1,0:T(8,128)(2,1)S(1)} %bitcast.64), channel_id=1, source_target_pairs={{0,1},{1,0},{2,3},{3,2},{4,5},{5,4},{6,7},{7,6},{8,9},{9,8},{10,11... | collective-permute-start | bytes 1572872 | tf_op jit(solution)/shard_map/ppermute | solution.py:154
  186.8 15.2 %collective-permute-start.12 = (bf16[1,256,1024]{2,1,0:T(8,128)(2,1)}, bf16[1,256,1024]{2,1,0:T(8,128)(2,1)S(1)}, u32[]{:S(2)}, u32[]{:S(2)}) collective-permute-start(bf16[1,256,1024]{2,1,0:T(8,128)(2,1)} %bitcast.77), channel_id=1, source_target_pairs={{0,4},{4,8},{8,12},{12,0},{1,5},{5,9},{9,13},{13,1},{2,6},{6,10},{... | collective-permute-start | bytes 1572872 | tf_op jit(solution)/shard_map/ppermute | solution.py:163
  188.4 26.0 %collective-permute-start.13 = (bf16[1,256,1024]{2,1,0:T(8,128)(2,1)}, bf16[1,256,1024]{2,1,0:T(8,128)(2,1)S(1)}, u32[]{:S(2)}, u32[]{:S(2)}) collective-permute-start(bf16[1,256,1024]{2,1,0:T(8,128)(2,1)} %bitcast.76), channel_id=1, source_target_pairs={{0,8},{4,12},{8,0},{12,4},{1,9},{5,13},{9,1},{13,5},{2,10},{6,14},... | collective-permute-start | bytes 1572872 | tf_op jit(solution)/shard_map/ppermute | solution.py:163
  191.3 23.1 %collective-permute-start.14 = (bf16[1,256,1024]{2,1,0:T(8,128)(2,1)}, bf16[1,256,1024]{2,1,0:T(8,128)(2,1)}, u32[]{:S(2)}, u32[]{:S(2)}) collective-permute-start(bf16[1,256,1024]{2,1,0:T(8,128)(2,1)} %bitcast.75), channel_id=1, source_target_pairs={{0,12},{4,0},{8,4},{12,8},{1,13},{5,1},{9,5},{13,9},{2,14},{6,2},{... | collective-permute-start | bytes 1572872 | tf_op jit(solution)/shard_map/ppermute | solution.py:163
  199.9 18.3 %copy-start.5 = (bf16[1,8,128,8,128]{4,3,2,1,0:T(8,128)(2,1)S(1)}, bf16[1,8,128,8,128]{4,3,2,1,0:T(8,128)(2,1)}, u32[]{:S(2)}) copy-start(bf16[1,8,128,8,128]{4,3,2,1,0:T(8,128)(2,1)} %get-tuple-element.54) | copy-start | bytes 6291460
  202.0 12.4 %copy-start.6 = (bf16[1,256,1024]{2,1,0:T(8,128)(2,1)}, bf16[1,256,1024]{2,1,0:T(8,128)(2,1)S(1)}, u32[]{:S(2)}) copy-start(bf16[1,256,1024]{2,1,0:T(8,128)(2,1)S(1)} %collective-permute-done.12.refs_1_) | copy-start | bytes 1572868
  214.4 0.8 copy-start.7
  225.4 4.7 %copy-start.4 = (f32[1024,1024]{1,0:T(8,128)S(1)}, f32[1024,1024]{1,0:T(8,128)}, u32[]{:S(2)}) copy-start(f32[1024,1024]{1,0:T(8,128)} %fusion.26) | copy-start | bytes 12582916
  230.1 2.1 copy-start.1
where the time goes:
time: 235 us; the launch traced here: 232 us
  between operations  80 us (34%)
  waiting for transfers between devices  56.4 us (24%)
  matrix products  30.8 us (13%)
  starting transfers between devices  30 us (13%)
  local copies, waits for them, and re-layouts  17.5 us (7%)
  Pallas kernels  13.8 us (6%)
  other arithmetic  3.68 us (2%)
    ppermute x6, waiting for transfers between devices, shift(): lax.ppermute(value, axis, [(i, (i + step) % count) for i in range(count)])  34.6 us
    all_to_all x2, waiting for transfers between devices, exchange(): return lax.all_to_all(value, axis, split_axis=0, concat_axis=0, tiled=True)  21.8 us
    all_to_all x2, starting transfers between devices, exchange(): return lax.all_to_all(value, axis, split_axis=0, concat_axis=0, tiled=True)  14.9 us
    dot_general x2, matrix products, right_product(): lax.dot_general(left, dense_block, (((1,), (1,)), ((), ())), preferred_el...  14.4 us
    ppermute x6, starting transfers between devices, shift(): lax.ppermute(value, axis, [(i, (i + step) % count) for i in range(count)])  12.5 us
    pallas_call x3, Pallas kernels, copy_pieces(): pl.pallas_call(kernel, out_shape=[jax.ShapeDtypeStruct(piece, pools[0].dt...  9.33 us
    dot_general x2, matrix products, expand(): jnp.einsum('rskc,rskij->sricj', onehot, blocks, preferred_element_type=jn...  7.45 us
    cond x4, local copies, waits for them, and re-layouts  5.46 us
  transfers between devices with their start and end apart: 13, of which 6 were waited for; matrix products, arithmetic and copies ran while one was open for 19% of the time, Pallas kernels for 6%

commit v1 on v0

--- a/solution.py
+++ b/solution.py
@@ -7,29 +7,107 @@
 from jax.sharding import PartitionSpec as P
 
 
-def expand(blocks, cols):
-    block_count = blocks.shape[0]
-    block_size = blocks.shape[3]
-    onehot = (cols[..., None] == jnp.arange(block_count, dtype=jnp.int32)).astype(jnp.bfloat16)
-    dense_rows = jnp.einsum("rskc,rskij->sricj", onehot, blocks, preferred_element_type=jnp.float32)
-    return dense_rows.reshape(2, block_count * block_size, block_count * block_size).astype(
-        jnp.bfloat16
-    )
-
-
-def right_product(left, dense_block):
-    return lax.dot_general(
-        left, dense_block, (((1,), (1,)), ((), ())), preferred_element_type=jnp.float32
-    )
-
-
-def copy_pieces(pools, table, count, codes):
+def fill(dense, blocks, table, pair, transpose):
+    dense[...] = jnp.zeros_like(dense)
+    size = blocks.shape[-1]
+    for row in range(blocks.shape[0]):
+        for k in range(blocks.shape[2]):
+            column = table[(row * 2 + pair) * blocks.shape[2] + k]
+            place = pl.ds(pl.multiple_of(column * size, size), size)
+            strip = pl.ds(row * size, size)
+            if transpose:
+                dense[place, strip] = blocks[row, pair, k].T
+            else:
+                dense[strip, place] = blocks[row, pair, k]
+
+
+def own_terms(coeffs, alpha_blocks, alpha_cols, beta_blocks, beta_cols):
+    size = coeffs.shape[0]
+    step = 256
+
+    def kernel(a_table, b_table, c, a_blocks, b_blocks, terms, a_listed, b_listed, a_own, b_own):
+        fill(a_own, a_blocks, a_table, 0, False)
+        fill(b_own, b_blocks, b_table, 0, True)
+        fill(a_listed, a_blocks, a_table, 1, False)
+        fill(b_listed, b_blocks, b_table, 1, True)
+
+        @pl.loop(0, size // step)
+        def _(i):
+            rows = pl.ds(pl.multiple_of(i * step, step), step)
+            terms[rows, :] = jnp.dot(
+                a_own[rows, :], c[...], preferred_element_type=jnp.float32
+            ) + jnp.dot(c[rows, :], b_own[...], preferred_element_type=jnp.float32)
+
+    square = (size, size)
+    whole = pl.BlockSpec(memory_space=pltpu.VMEM)
+    return pl.pallas_call(
+        kernel,
+        out_shape=[
+            jax.ShapeDtypeStruct(square, jnp.float32),
+            jax.ShapeDtypeStruct(square, jnp.bfloat16),
+            jax.ShapeDtypeStruct(square, jnp.bfloat16),
+        ],
+        in_specs=[pl.BlockSpec(memory_space=pltpu.SMEM)] * 2 + [whole] * 3,
+        out_specs=[whole] * 3,
+        scratch_shapes=[pltpu.VMEM(square, jnp.bfloat16)] * 2,
+        cost_estimate=pl.CostEstimate(
+            flops=4 * size**3, transcendentals=0, bytes_accessed=15 * size * size
+        ),
+    )(alpha_cols.reshape(-1), beta_cols.reshape(-1), coeffs, alpha_blocks, beta_blocks)
+
+
+def add_beta(table, terms, pieces, dense):
+    step, size = pieces[0].shape
+
+    def kernel(table_ref, terms_ref, dense_ref, *refs):
+        pieces_ref, out = refs[:-1], refs[-1]
+        for i, block in enumerate(order_codes(table_ref)):
+            rows = pl.ds(pl.multiple_of(block * step, step), step)
+            out[rows, :] = terms_ref[rows, :] + jnp.dot(
+                pieces_ref[i][...], dense_ref[...], preferred_element_type=jnp.float32
+            )
+
+    whole = pl.BlockSpec(memory_space=pltpu.VMEM)
+    return pl.pallas_call(
+        kernel,
+        out_shape=jax.ShapeDtypeStruct(terms.shape, jnp.float32),
+        in_specs=[pl.BlockSpec(memory_space=pltpu.SMEM)] + [whole] * (2 + len(pieces)),
+        out_specs=whole,
+        input_output_aliases={1: 0},
+        cost_estimate=pl.CostEstimate(
+            flops=2 * size**3, transcendentals=0, bytes_accessed=12 * size * size
+        ),
+    )(table, terms, dense, *pieces)
+
+
+def add_alpha(terms, dense, fetched):
+    size = terms.shape[0]
+    step = 256
+
+    def kernel(terms_ref, dense_ref, fetched_ref, out):
+        product = jnp.dot(dense_ref[...], fetched_ref[...], preferred_element_type=jnp.float32)
+        out[...] = (terms_ref[...] + product).astype(out.dtype)
+
+    strip = pl.BlockSpec((size, step), lambda i: (0, i))
+    return pl.pallas_call(
+        kernel,
+        out_shape=jax.ShapeDtypeStruct(terms.shape, fetched.dtype),
+        grid=(size // step,),
+        in_specs=[strip, pl.BlockSpec((size, size), lambda i: (0, 0)), strip],
+        out_specs=strip,
+        cost_estimate=pl.CostEstimate(
+            flops=2 * size**3, transcendentals=0, bytes_accessed=10 * size * size
+        ),
+    )(terms, dense, fetched)
+
+
+def copy_pieces(pools, table, count, codes, tally=False):
     piece = pools[0].shape[1:]
 
     def kernel(table_ref, *refs):
         sources = refs[: len(pools)]
         outs = refs[len(pools) : len(pools) + count]
-        held, in_sem, out_sem = refs[len(pools) + count :]
+        held, in_sem, out_sem = refs[-3:]
         for i, (pool, index) in enumerate(codes(table_ref)):
             for c, source in enumerate(sources):
 
@@ -39,6 +117,9 @@
                         source.at[jnp.minimum(index, source.shape[0] - 1)], held.at[i], in_sem.at[i]
                     ).start()
 
+        if tally:
+            sides = [sum(crossing(table_ref, side, 1 - side)) for side in (0, 1)]
+            refs[len(pools) + count][0] = jnp.maximum(sides[0], sides[1])
         for i in range(count):
             pltpu.make_async_copy(sources[0].at[0], held.at[i], in_sem.at[i]).wait()
             pltpu.make_async_copy(held.at[i], outs[i], out_sem.at[i]).start()
@@ -47,12 +128,14 @@
 
     return pl.pallas_call(
         kernel,
-        out_shape=[jax.ShapeDtypeStruct(piece, pools[0].dtype)] * count,
+        out_shape=[jax.ShapeDtypeStruct(piece, pools[0].dtype)] * count
+        + [jax.ShapeDtypeStruct((1,), jnp.int32)] * tally,
         grid_spec=pltpu.PrefetchScalarGridSpec(
             num_scalar_prefetch=1,
             grid=(1,),
             in_specs=[pl.BlockSpec(memory_space=pl.ANY)] * len(pools),
-            out_specs=[pl.BlockSpec(memory_space=pl.ANY)] * count,
+            out_specs=[pl.BlockSpec(memory_space=pl.ANY)] * count
+            + [pl.BlockSpec(memory_space=pltpu.SMEM)] * tally,
             scratch_shapes=[
                 pltpu.VMEM((count,) + piece, pools[0].dtype),
                 pltpu.SemaphoreType.DMA((count,)),
@@ -63,6 +146,14 @@
             flops=0, transcendentals=0, bytes_accessed=4 * count * piece[0] * piece[1]
         ),
     )(table, *pools)
+
+
+def unwritten(count, shape, dtype):
+    return pl.pallas_call(
+        lambda *refs: None,
+        out_shape=[jax.ShapeDtypeStruct(shape, dtype)] * count,
+        out_specs=[pl.BlockSpec(memory_space=pl.ANY)] * count,
+    )()
 
 
 def gather_pieces(pool, table):
@@ -147,7 +238,7 @@
 def order_codes(table):
     y, z_lo, core = place()
     mine = table[4 * y + 2 * z_lo + core] // 4
-    return [((y - mine - i + 8) % 4, jnp.int32(0)) for i in range(4)]
+    return [(y - mine - i + 8) % 4 for i in range(4)]
 
 
 def swap(value, axis):
@@ -174,38 +265,34 @@
     alpha_held = exchange(alpha_pieces, ("zh", "x"))
 
     near_twin = swap(near, "core")
-    slots = copy_pieces([near, near_twin], beta_list, 2, slot_codes(0))
+    *slots, most = copy_pieces([near, near_twin], beta_list, 2, slot_codes(0), tally=True)
     slots = [swap(slot, "zl")[None] for slot in slots]
-    slots = [[slot, swap(slot, "core")] for slot in slots]
-
-    counts = [sum(crossing(beta_list, side, 1 - side)) for side in (0, 1)]
 
     def carry():
         more = copy_pieces([near, near_twin], beta_list, 2, slot_codes(2))
-        more = [swap(slot, "zl")[None] for slot in more]
-        return [[slot, swap(slot, "core")] for slot in more]
+        more = [swap(slot, "zl") for slot in more]
+        return tuple(more + [swap(slot, "core") for slot in more])
 
     def skip():
-        return slots
-
-    more = lax.cond(jnp.maximum(counts[0], counts[1]) > 4, carry, skip)
-    pools = [near, near_twin] + slots[0] + slots[1] + more[0] + more[1]
-    leaving = [piece[None] for piece in copy_pieces(pools, beta_list, 4, send_codes)]
-    arrived = leaving[:1] + [shift(leaving[s], "y", s) for s in (1, 2, 3)]
-    beta_fetched = copy_pieces(arrived, beta_list, 4, order_codes)
+        return tuple(unwritten(4, near.shape[1:], near.dtype))
+
+    more = lax.cond(most[0] > 4, carry, skip)
+    pools = [near, near_twin]
+    for slot in slots:
+        pools += [slot, swap(slot, "core")]
+    for own, twin in zip(more[:2], more[2:]):
+        pools += [own[None], twin[None]]
+    leaving = copy_pieces(pools, beta_list, 4, send_codes)
+    arrived = [leaving[0]] + [shift(leaving[s], "y", s) for s in (1, 2, 3)]
 
     alpha_out = gather_pieces(alpha_held, alpha_list)
     alpha_fetched = exchange(alpha_out, ("zh", "x")).reshape(strings, strings)
 
-    alpha_dense = expand(alpha_blocks, alpha_cols)
-    beta_dense = expand(beta_blocks, beta_cols)
-    terms = jnp.dot(alpha_dense[0], coeffs, preferred_element_type=jnp.float32)
-    terms = terms + right_product(coeffs, beta_dense[0])
-    terms = lax.optimization_barrier(terms)
-    terms = terms + right_product(jnp.concatenate(beta_fetched), beta_dense[1])
-    terms = lax.optimization_barrier(terms)
-    terms = terms + jnp.dot(alpha_dense[1], alpha_fetched, preferred_element_type=jnp.float32)
-    return terms.astype(jnp.bfloat16)
+    terms, alpha_dense, beta_dense = own_terms(
+        coeffs, alpha_blocks, alpha_cols, beta_blocks, beta_cols
+    )
+    terms = add_beta(beta_list, terms, arrived, beta_dense)
+    return add_alpha(terms, alpha_dense, alpha_fetched)
 
 
 def solution(mesh):

time: 235 us -> 190 us (0.81)
  between operations: 80 us -> 0.7 us
  waiting for transfers between devices: 56.4 us -> 116 us
  matrix products: 30.8 us -> 0 us
  Pallas kernels: 13.8 us -> 37.6 us
  local copies, waits for them, and re-layouts: 17.5 us -> 4.76 us
    ppermute x5, waiting for transfers between devices: 0.01 us -> 62 us  [swap(): return lax.ppermute(value, axis, [(0, 1), (1, 0)])]
    dot_general x6 -> x0, matrix products: 30.8 us -> none  [the longest x2 14.4 us: right_product(): lax.dot_general(left, dense_block, (((1,), (1,)), ((), ())), preferred_el...]
    pallas_call x0 -> x4, Pallas kernels: none -> 26.6 us  [the longest x1 12.3 us: own_terms(): pl.pallas_call(kernel, out_shape=[jax.ShapeDtypeStruct(square, jnp.float3...]
    ppermute x6, waiting for transfers between devices: 34.6 us -> 8.12 us  [shift(): lax.ppermute(value, axis, [(i, (i + step) % count) for i in range(count)])]
    all_to_all x2, waiting for transfers between devices: 21.8 us -> 45.4 us  [exchange(): return lax.all_to_all(value, axis, split_axis=0, concat_axis=0, tiled=True)]
    slice x3 -> x0, local copies, waits for them, and re-layouts: 9.33 us -> none  [the longest x1 4.57 us: sigma(): terms = terms + right_product(jnp.concatenate(beta_fetched), beta_dense[1])]
    cond x4 -> x0, local copies, waits for them, and re-layouts: 5.46 us -> none
    pallas_call x3 -> x2, Pallas kernels: 9.33 us -> 6.42 us  [copy_pieces(): pl.pallas_call(kernel, out_shape=[jax.ShapeDtypeStruct(piece, pools[0].dt...]
  transfers between devices with their start and end apart: 13 -> 13, of which waited for: 6 -> 6; matrix products, arithmetic and copies ran while one was open for 19% -> 2% of each run, Pallas kernels for 6% -> 16%
where the time goes in v1:
time: 190 us; the launch traced here: 189 us
  waiting for transfers between devices  116 us (61%)
  Pallas kernels  37.6 us (20%)
  starting transfers between devices  28.6 us (15%)
  local copies, waits for them, and re-layouts  4.76 us (3%)
    ppermute x5, waiting for transfers between devices, swap(): return lax.ppermute(value, axis, [(0, 1), (1, 0)])  62 us
    all_to_all x2, waiting for transfers between devices, exchange(): return lax.all_to_all(value, axis, split_axis=0, concat_axis=0, tiled=True)  45.4 us
    all_to_all x2, starting transfers between devices, exchange(): return lax.all_to_all(value, axis, split_axis=0, concat_axis=0, tiled=True)  14.8 us
    pallas_call x1, Pallas kernels, own_terms(): pl.pallas_call(kernel, out_shape=[jax.ShapeDtypeStruct(square, jnp.float3...  12.3 us
    ppermute x6, starting transfers between devices, shift(): lax.ppermute(value, axis, [(i, (i + step) % count) for i in range(count)])  11.6 us
    ppermute x6, waiting for transfers between devices, shift(): lax.ppermute(value, axis, [(i, (i + step) % count) for i in range(count)])  8.12 us
    pallas_call x1, Pallas kernels, add_beta(): pl.pallas_call(kernel, out_shape=jax.ShapeDtypeStruct(terms.shape, jnp.fl...  7.64 us
    pallas_call x1, Pallas kernels, add_alpha(): pl.pallas_call(kernel, out_shape=jax.ShapeDtypeStruct(terms.shape, fetche...  6.75 us
  transfers between devices with their start and end apart: 13, of which 6 were waited for; matrix products, arithmetic and copies ran while one was open for 2% of the time, Pallas kernels for 16%

profile of v1, /device:TPU:32, one launch (start us, length us, event | category | flops | bytes accessed | tf_op | source)
XLA Modules:
  0.0 188.6 jit_solution(1756890629544345459)
XLA Ops:
  0.0 10.3 %all-to-all-start = ((bf16[16,64,1024]{2,1,0:T(8,128)(2,1)}), bf16[16,64,1024]{2,1,0:T(8,128)(2,1)}, u32[]{:S(2)}, u32[]{:S(2)}) async-start(bf16[16,64,1024]{2,1,0:T(8,128)(2,1)} %bitcast.18), calls=%async_computation | async-start | bytes 4194304 | tf_op jit(solution)/shard_map/all_to_all | solution.py:249
  10.3 1.2 slice_bitcast_fusion
  11.5 3.2 %collective-permute-start.5 = (bf16[256,1024]{1,0:T(8,128)(2,1)}, bf16[256,1024]{1,0:T(8,128)(2,1)S(1)}, u32[]{:S(2)}, u32[]{:S(2)}) collective-permute-start(bf16[256,1024]{1,0:T(8,128)(2,1)} %get-tuple-element.57), channel_id=1, source_target_pairs={{0,8},{4,12},{8,0},{12,4},{1,9},{5,13},{9,1},{13,5},{2,10},{6,14},... | collective-permute-start | bytes 1572872 | tf_op jit(solution)/shard_map/ppermute | solution.py:254
  14.7 1.1 collective-permute-start.6
  15.8 1.0 collective-permute-start.4
  16.7 45.4 %all-to-all-done.source = bf16[16,64,1024]{2,1,0:T(8,128)(2,1)} async-done(((bf16[16,64,1024]{2,1,0:T(8,128)(2,1)}), bf16[16,64,1024]{2,1,0:T(8,128)(2,1)}, u32[]{:S(2)}, u32[]{:S(2)}) %all-to-all-start) | async-done | bytes 2097184 | tf_op jit(solution)/shard_map/all_to_all | solution.py:249
  62.1 4.6 %shard_map.77 = bf16[16,64,1024]{2,1,0:T(8,128)(2,1)} custom-call(s32[16]{0:T(128)} %table_ref.7, bf16[16,64,1024]{2,1,0:T(8,128)(2,1)} %all-to-all-done.source), custom_call_target="tpu_custom_call" | custom-call | bytes 4194304 | tf_op jit(solution)/shard_map/pallas_call | solution.py:171
  66.6 4.5 %all-to-all-start.1 = ((bf16[16,64,1024]{2,1,0:T(8,128)(2,1)}), bf16[16,64,1024]{2,1,0:T(8,128)(2,1)}, u32[]{:S(2)}, u32[]{:S(2)}) async-start(bf16[16,64,1024]{2,1,0:T(8,128)(2,1)} %shard_map.77), calls=%async_computation.1 | async-start | bytes 4194304 | tf_op jit(solution)/shard_map/all_to_all | solution.py:249
  72.1 1.5 pad_maximum_fusion.refs_0_
  73.7 4.3 %collective-permute-done.7.refs_1_ = bf16[4,256,1024]{2,1,0:T(8,128)(2,1)} collective-permute-done((bf16[4,256,1024]{2,1,0:T(8,128)(2,1)S(1)}, bf16[4,256,1024]{2,1,0:T(8,128)(2,1)}, u32[]{:S(2)}, u32[]{:S(2)}) %collective-permute-start.7) | collective-permute-done | bytes 2097184 | tf_op jit(solution)/shard_map/ppermute | solution.py:245
  78.0 3.2 %shard_map.74 = (bf16[256,1024]{1,0:T(8,128)(2,1)}, bf16[256,1024]{1,0:T(8,128)(2,1)}, s32[1]{0:T(128)}) custom-call(s32[16]{0:T(128)S(1)} %copy-done.12, bf16[4,256,1024]{2,1,0:T(8,128)(2,1)S(1)} %pad_maximum_fusion.refs_0_, bf16[4,256,1024]{2,1,0:T(8,128)(2,1)} %collective-permute-done.7.refs_1_), custom_call_target="tpu_custom_call" | custom-call | bytes 2097152 | tf_op jit(solution)/shard_map/pallas_call | solution.py:129
  81.2 1.1 collective-permute-start.10
  82.3 1.0 collective-permute-start.8
  83.3 46.6 %collective-permute-done.10 = bf16[256,1024]{1,0:T(8,128)(2,1)S(1)} collective-permute-done((bf16[256,1024]{1,0:T(8,128)(2,1)}, bf16[256,1024]{1,0:T(8,128)(2,1)S(1)}, u32[]{:S(2)}, u32[]{:S(2)}) %collective-permute-start.10) | collective-permute-done | bytes 524320 | tf_op jit(solution)/shard_map/ppermute | solution.py:245
  129.9 9.9 %collective-permute-done.8 = bf16[256,1024]{1,0:T(8,128)(2,1)S(1)} collective-permute-done((bf16[256,1024]{1,0:T(8,128)(2,1)}, bf16[256,1024]{1,0:T(8,128)(2,1)S(1)}, u32[]{:S(2)}, u32[]{:S(2)}) %collective-permute-start.8) | collective-permute-done | bytes 524320 | tf_op jit(solution)/shard_map/ppermute | solution.py:245
  140.6 1.2 collective-permute-done.9.refs_3_
  141.8 3.2 %shard_map.75 = (bf16[256,1024]{1,0:T(8,128)(2,1)}, bf16[256,1024]{1,0:T(8,128)(2,1)}, bf16[256,1024]{1,0:T(8,128)(2,1)}, bf16[256,1024]{1,0:T(8,128)(2,1)}) custom-call(s32[16]{0:T(128)S(1)} %copy-done.12, bf16[4,256,1024]{2,1,0:T(8,128)(2,1)S(1)} %pad_maximum_fusion.refs_0_, bf16[4,256,1024]{2,1,0:T(8,128)(2,1)} %collective-permute-done.7.refs_1_, ...), custom_call_target="tpu_custom_call" | custom-call | bytes 4194304 | tf_op jit(solution)/shard_map/pallas_call | solution.py:129
  145.1 2.0 %collective-permute-start.12 = (bf16[256,1024]{1,0:T(8,128)(2,1)}, bf16[256,1024]{1,0:T(8,128)(2,1)S(1)}, u32[]{:S(2)}, u32[]{:S(2)}) collective-permute-start(bf16[256,1024]{1,0:T(8,128)(2,1)} %get-tuple-element.52), channel_id=1, source_target_pairs={{0,4},{4,8},{8,12},{12,0},{1,5},{5,9},{9,13},{13,1},{2,6},{6,10},{... | collective-permute-start | bytes 1572872 | tf_op jit(solution)/shard_map/ppermute | solution.py:254
  147.1 2.7 %collective-permute-start.13 = (bf16[256,1024]{1,0:T(8,128)(2,1)}, bf16[256,1024]{1,0:T(8,128)(2,1)S(1)}, u32[]{:S(2)}, u32[]{:S(2)}) collective-permute-start(bf16[256,1024]{1,0:T(8,128)(2,1)} %get-tuple-element.53), channel_id=1, source_target_pairs={{0,8},{4,12},{8,0},{12,4},{1,9},{5,13},{9,1},{13,5},{2,10},{6,14},... | collective-permute-start | bytes 1572872 | tf_op jit(solution)/shard_map/ppermute | solution.py:254
  149.8 1.6 collective-permute-start.14
  152.9 12.3 %shard_map.73 = (f32[1024,1024]{1,0:T(8,128)}, bf16[1024,1024]{1,0:T(8,128)(2,1)}, bf16[1024,1024]{1,0:T(8,128)(2,1)}) custom-call(s32[80]{0:T(128)} %reshape.24.a_table, s32[80]{0:T(128)} %reshape.25.b_table, bf16[1024,1024]{1,0:T(8,128)(2,1)} %c.1, bf16[8,2,5,128,128]{4,3,2,1,0:T(8,128)(2,1)} %a_blocks.1, bf16[8,2,5,128,128]{4,3,2,1,0:T(8,128)(2,1)} %b_blocks.1), custom_call_target="tpu_custom_call" | custom-call | flops 4294967296 | bytes 15728640 | tf_op jit(solution)/shard_map/pallas_call | solution.py:43
  165.1 8.1 %collective-permute-done.13.refs_2_ = bf16[256,1024]{1,0:T(8,128)(2,1)S(1)} collective-permute-done((bf16[256,1024]{1,0:T(8,128)(2,1)}, bf16[256,1024]{1,0:T(8,128)(2,1)S(1)}, u32[]{:S(2)}, u32[]{:S(2)}) %collective-permute-start.13) | collective-permute-done | bytes 524320 | tf_op jit(solution)/shard_map/ppermute | solution.py:254
  174.2 7.6 %shard_map.76.terms_ref = f32[1024,1024]{1,0:T(8,128)} custom-call(s32[16]{0:T(128)S(1)} %copy-done.12, f32[1024,1024]{1,0:T(8,128)} %get-tuple-element.42.terms_ref, bf16[1024,1024]{1,0:T(8,128)(2,1)} %get-tuple-element.43.dense_ref, bf16[256,1024]{1,0:T(8,128)(2,1)} %get-tuple-element.51.refs_0_, ...), custom_call_target="tpu_custom_call", output_to_operand_aliasing={{}: (1, {})} | custom-call | flops 2147483648 | bytes 12582912 | tf_op jit(solution)/shard_map/pallas_call | solution.py:71
  181.9 6.8 %shard_map.78 = bf16[1024,1024]{1,0:T(8,128)(2,1)} custom-call(f32[1024,1024]{1,0:T(8,128)} %shard_map.76.terms_ref, bf16[1024,1024]{1,0:T(8,128)(2,1)} %get-tuple-element.55.dense_ref, bf16[1024,1024]{1,0:T(8,128)(2,1)} %bitcast.16.fetched_ref), custom_call_target="tpu_custom_call" | custom-call | flops 2147483648 | bytes 10485760 | tf_op jit(solution)/shard_map/pallas_call | solution.py:92
  (38 shorter events, 3.7 us)
Async XLA Ops:
  0.0 10.3 %copy-start = (bf16[1024,1024]{1,0:T(8,128)(2,1)S(1)}, bf16[1024,1024]{1,0:T(8,128)(2,1)}, u32[]{:S(2)}) copy-start(bf16[1024,1024]{1,0:T(8,128)(2,1)} %c.1) | copy-start | bytes 6291460
  0.0 62.1 %all-to-all-start = ((bf16[16,64,1024]{2,1,0:T(8,128)(2,1)}), bf16[16,64,1024]{2,1,0:T(8,128)(2,1)}, u32[]{:S(2)}, u32[]{:S(2)}) async-start(bf16[16,64,1024]{2,1,0:T(8,128)(2,1)} %bitcast.18), calls=%async_computation | async-start | bytes 4194304 | tf_op jit(solution)/shard_map/all_to_all | solution.py:249
  11.5 59.6 %collective-permute-start.5 = (bf16[256,1024]{1,0:T(8,128)(2,1)}, bf16[256,1024]{1,0:T(8,128)(2,1)S(1)}, u32[]{:S(2)}, u32[]{:S(2)}) collective-permute-start(bf16[256,1024]{1,0:T(8,128)(2,1)} %get-tuple-element.57), channel_id=1, source_target_pairs={{0,8},{4,12},{8,0},{12,4},{1,9},{5,13},{9,1},{13,5},{2,10},{6,14},... | collective-permute-start | bytes 1572872 | tf_op jit(solution)/shard_map/ppermute | solution.py:254
  14.7 56.4 %collective-permute-start.6 = (bf16[256,1024]{1,0:T(8,128)(2,1)}, bf16[256,1024]{1,0:T(8,128)(2,1)S(1)}, u32[]{:S(2)}, u32[]{:S(2)}) collective-permute-start(bf16[256,1024]{1,0:T(8,128)(2,1)} %get-tuple-element.59), channel_id=1, source_target_pairs={{0,12},{4,0},{8,4},{12,8},{1,13},{5,1},{9,5},{13,9},{2,14},{6,2},{... | collective-permute-start | bytes 1572872 | tf_op jit(solution)/shard_map/ppermute | solution.py:254
  15.8 55.4 %collective-permute-start.4 = (bf16[256,1024]{1,0:T(8,128)(2,1)}, bf16[256,1024]{1,0:T(8,128)(2,1)S(1)}, u32[]{:S(2)}, u32[]{:S(2)}) collective-permute-start(bf16[256,1024]{1,0:T(8,128)(2,1)} %get-tuple-element.58), channel_id=1, source_target_pairs={{0,4},{4,8},{8,12},{12,0},{1,5},{5,9},{9,13},{13,1},{2,6},{6,10},{... | collective-permute-start | bytes 1572872 | tf_op jit(solution)/shard_map/ppermute | solution.py:254
  66.6 115.2 %all-to-all-start.1 = ((bf16[16,64,1024]{2,1,0:T(8,128)(2,1)}), bf16[16,64,1024]{2,1,0:T(8,128)(2,1)}, u32[]{:S(2)}, u32[]{:S(2)}) async-start(bf16[16,64,1024]{2,1,0:T(8,128)(2,1)} %shard_map.77), calls=%async_computation.1 | async-start | bytes 4194304 | tf_op jit(solution)/shard_map/all_to_all | solution.py:249
  71.1 0.8 copy-start.10
  71.2 0.9 copy-start.11
  72.1 5.9 %copy-start.12 = (s32[16]{0:T(128)S(1)}, s32[16]{0:T(128)}, u32[]{:S(2)}) copy-start(s32[16]{0:T(128)} %table_ref.6) | copy-start | bytes 196
  73.6 4.4 %collective-permute-start.7 = (bf16[4,256,1024]{2,1,0:T(8,128)(2,1)S(1)}, bf16[4,256,1024]{2,1,0:T(8,128)(2,1)}, u32[]{:S(2)}, u32[]{:S(2)}) collective-permute-start(bf16[4,256,1024]{2,1,0:T(8,128)(2,1)S(1)} %pad_maximum_fusion.refs_0_), channel_id=1, source_target_pairs={{0,1},{1,0},{2,3},{3,2},{4,5},{5,4},{6,7},{7,6},{8,9},{9,8},{10,11... | collective-permute-start | bytes 6291464 | tf_op jit(solution)/shard_map/ppermute | solution.py:245
  81.2 48.7 %collective-permute-start.10 = (bf16[256,1024]{1,0:T(8,128)(2,1)}, bf16[256,1024]{1,0:T(8,128)(2,1)S(1)}, u32[]{:S(2)}, u32[]{:S(2)}) collective-permute-start(bf16[256,1024]{1,0:T(8,128)(2,1)} %get-tuple-element.45), channel_id=1, source_target_pairs={{0,2},{2,0},{1,3},{3,1},{4,6},{6,4},{5,7},{7,5},{8,10},{10,8},{9,1... | collective-permute-start | bytes 1572872 | tf_op jit(solution)/shard_map/ppermute | solution.py:245
  82.3 57.5 %collective-permute-start.8 = (bf16[256,1024]{1,0:T(8,128)(2,1)}, bf16[256,1024]{1,0:T(8,128)(2,1)S(1)}, u32[]{:S(2)}, u32[]{:S(2)}) collective-permute-start(bf16[256,1024]{1,0:T(8,128)(2,1)} %get-tuple-element.44), channel_id=1, source_target_pairs={{0,2},{2,0},{1,3},{3,1},{4,6},{6,4},{5,7},{7,5},{8,10},{10,8},{9,1... | collective-permute-start | bytes 1572872 | tf_op jit(solution)/shard_map/ppermute | solution.py:245
  129.9 10.4 %copy-start.1 = (bf16[256,1024]{1,0:T(8,128)(2,1)}, bf16[256,1024]{1,0:T(8,128)(2,1)S(1)}, u32[]{:S(2)}) copy-start(bf16[256,1024]{1,0:T(8,128)(2,1)S(1)} %collective-permute-done.10) | copy-start | bytes 1572868
  129.9 10.7 %collective-permute-start.11 = (bf16[1,256,1024]{2,1,0:T(8,128)(2,1)S(1)}, bf16[1,256,1024]{2,1,0:T(8,128)(2,1)}, u32[]{:S(2)}, u32[]{:S(2)}) collective-permute-start(bf16[1,256,1024]{2,1,0:T(8,128)(2,1)S(1)} %bitcast.19), channel_id=1, source_target_pairs={{0,1},{1,0},{2,3},{3,2},{4,5},{5,4},{6,7},{7,6},{8,9},{9,8},{10,11... | collective-permute-start | bytes 1572872 | tf_op jit(solution)/shard_map/ppermute | solution.py:245
  139.8 0.8 copy-start.2
  139.8 2.0 %collective-permute-start.9 = (bf16[1,256,1024]{2,1,0:T(8,128)(2,1)S(1)}, bf16[1,256,1024]{2,1,0:T(8,128)(2,1)}, u32[]{:S(2)}, u32[]{:S(2)}) collective-permute-start(bf16[1,256,1024]{2,1,0:T(8,128)(2,1)S(1)} %bitcast.21), channel_id=1, source_target_pairs={{0,1},{1,0},{2,3},{3,2},{4,5},{5,4},{6,7},{7,6},{8,9},{9,8},{10,11... | collective-permute-start | bytes 1572872 | tf_op jit(solution)/shard_map/ppermute | solution.py:245
  141.8 9.6 %copy-start.13 = (s32[8,2,5]{0,1,2:T(2,128)S(1)}, s32[8,2,5]{0,1,2:T(2,128)}, u32[]{:S(2)}) copy-start(s32[8,2,5]{0,1,2:T(2,128)} %param.11) | copy-start | bytes 964
  141.8 10.3 %copy-start.14 = (s32[8,2,5]{0,1,2:T(2,128)S(1)}, s32[8,2,5]{0,1,2:T(2,128)}, u32[]{:S(2)}) copy-start(s32[8,2,5]{0,1,2:T(2,128)} %param.14) | copy-start | bytes 964
  145.1 20.1 %collective-permute-start.12 = (bf16[256,1024]{1,0:T(8,128)(2,1)}, bf16[256,1024]{1,0:T(8,128)(2,1)S(1)}, u32[]{:S(2)}, u32[]{:S(2)}) collective-permute-start(bf16[256,1024]{1,0:T(8,128)(2,1)} %get-tuple-element.52), channel_id=1, source_target_pairs={{0,4},{4,8},{8,12},{12,0},{1,5},{5,9},{9,13},{13,1},{2,6},{6,10},{... | collective-permute-start | bytes 1572872 | tf_op jit(solution)/shard_map/ppermute | solution.py:254
  147.1 26.1 %collective-permute-start.13 = (bf16[256,1024]{1,0:T(8,128)(2,1)}, bf16[256,1024]{1,0:T(8,128)(2,1)S(1)}, u32[]{:S(2)}, u32[]{:S(2)}) collective-permute-start(bf16[256,1024]{1,0:T(8,128)(2,1)} %get-tuple-element.53), channel_id=1, source_target_pairs={{0,8},{4,12},{8,0},{12,4},{1,9},{5,13},{9,1},{13,5},{2,10},{6,14},... | collective-permute-start | bytes 1572872 | tf_op jit(solution)/shard_map/ppermute | solution.py:254
  149.8 23.4 %collective-permute-start.14 = (bf16[256,1024]{1,0:T(8,128)(2,1)}, bf16[256,1024]{1,0:T(8,128)(2,1)S(1)}, u32[]{:S(2)}, u32[]{:S(2)}) collective-permute-start(bf16[256,1024]{1,0:T(8,128)(2,1)} %get-tuple-element.54), channel_id=1, source_target_pairs={{0,12},{4,0},{8,4},{12,8},{1,13},{5,1},{9,5},{13,9},{2,14},{6,2},{... | collective-permute-start | bytes 1572872 | tf_op jit(solution)/shard_map/ppermute | solution.py:254
  165.1 8.1 %copy-start.3 = (bf16[256,1024]{1,0:T(8,128)(2,1)}, bf16[256,1024]{1,0:T(8,128)(2,1)S(1)}, u32[]{:S(2)}) copy-start(bf16[256,1024]{1,0:T(8,128)(2,1)S(1)} %collective-permute-done.12.refs_1_) | copy-start | bytes 1572868
  173.2 0.8 copy-start.4
  173.2 1.0 copy-start.5

commit v2 on v1

--- a/solution.py
+++ b/solution.py
@@ -56,96 +56,112 @@
     )(alpha_cols.reshape(-1), beta_cols.reshape(-1), coeffs, alpha_blocks, beta_blocks)
 
 
-def add_beta(table, terms, pieces, dense):
+def add_beta(facts, terms, pieces, dense):
     step, size = pieces[0].shape
 
-    def kernel(table_ref, terms_ref, dense_ref, *refs):
-        pieces_ref, out = refs[:-1], refs[-1]
-        for i, block in enumerate(order_codes(table_ref)):
-            rows = pl.ds(pl.multiple_of(block * step, step), step)
-            out[rows, :] = terms_ref[rows, :] + jnp.dot(
-                pieces_ref[i][...], dense_ref[...], preferred_element_type=jnp.float32
-            )
-
-    whole = pl.BlockSpec(memory_space=pltpu.VMEM)
+    def kernel(facts_ref, terms_ref, dense_ref, *refs):
+        out = refs[-1]
+        for i, piece in enumerate(refs[:-1]):
+
+            @pl.when(pl.program_id(0) == i)
+            def _():
+                out[...] = terms_ref[...] + jnp.dot(
+                    piece[...], dense_ref[...], preferred_element_type=jnp.float32
+                )
+
+    rows = pl.BlockSpec((step, size), lambda i, facts: (facts[1 + i], 0))
+    piece = pl.BlockSpec((step, size), lambda i, facts: (0, 0))
     return pl.pallas_call(
         kernel,
         out_shape=jax.ShapeDtypeStruct(terms.shape, jnp.float32),
-        in_specs=[pl.BlockSpec(memory_space=pltpu.SMEM)] + [whole] * (2 + len(pieces)),
-        out_specs=whole,
+        grid_spec=pltpu.PrefetchScalarGridSpec(
+            num_scalar_prefetch=1,
+            grid=(len(pieces),),
+            in_specs=[rows, pl.BlockSpec((size, size), lambda i, facts: (0, 0))]
+            + [piece] * len(pieces),
+            out_specs=rows,
+        ),
         input_output_aliases={1: 0},
         cost_estimate=pl.CostEstimate(
             flops=2 * size**3, transcendentals=0, bytes_accessed=12 * size * size
         ),
-    )(table, terms, dense, *pieces)
+    )(facts, terms, dense, *pieces)
 
 
 def add_alpha(terms, dense, fetched):
     size = terms.shape[0]
-    step = 256
+    step = size // 2
 
     def kernel(terms_ref, dense_ref, fetched_ref, out):
         product = jnp.dot(dense_ref[...], fetched_ref[...], preferred_element_type=jnp.float32)
         out[...] = (terms_ref[...] + product).astype(out.dtype)
 
-    strip = pl.BlockSpec((size, step), lambda i: (0, i))
+    rows = pl.BlockSpec((step, size), lambda i: (i, 0))
     return pl.pallas_call(
         kernel,
         out_shape=jax.ShapeDtypeStruct(terms.shape, fetched.dtype),
         grid=(size // step,),
-        in_specs=[strip, pl.BlockSpec((size, size), lambda i: (0, 0)), strip],
-        out_specs=strip,
+        in_specs=[rows, rows, pl.BlockSpec((size, size), lambda i: (0, 0))],
+        out_specs=rows,
         cost_estimate=pl.CostEstimate(
             flops=2 * size**3, transcendentals=0, bytes_accessed=10 * size * size
         ),
     )(terms, dense, fetched)
 
 
-def copy_pieces(pools, table, count, codes, tally=False):
-    piece = pools[0].shape[1:]
+def copy_pieces(parts, table, count, codes, tally=False):
+    rows, width = parts[0][0].shape
+    kind = parts[0][0].dtype
+    piece = (len(parts) * rows, width)
+    flat = sum((list(part) for part in parts), [])
 
     def kernel(table_ref, *refs):
-        sources = refs[: len(pools)]
-        outs = refs[len(pools) : len(pools) + count]
+        outs = refs[len(flat) : len(flat) + count]
         held, in_sem, out_sem = refs[-3:]
-        for i, (pool, index) in enumerate(codes(table_ref)):
-            for c, source in enumerate(sources):
+        for i, pool in enumerate(codes(table_ref)):
+            for c in range(len(parts[0])):
 
                 @pl.when(pool == c)
                 def _():
-                    pltpu.make_async_copy(
-                        source.at[jnp.minimum(index, source.shape[0] - 1)], held.at[i], in_sem.at[i]
-                    ).start()
+                    for h in range(len(parts)):
+                        pltpu.make_async_copy(
+                            refs[h * len(parts[0]) + c],
+                            held.at[i, pl.ds(h * rows, rows)],
+                            in_sem.at[i, h],
+                        ).start()
 
         if tally:
+            facts = refs[len(flat) + count]
             sides = [sum(crossing(table_ref, side, 1 - side)) for side in (0, 1)]
-            refs[len(pools) + count][0] = jnp.maximum(sides[0], sides[1])
-        for i in range(count):
-            pltpu.make_async_copy(sources[0].at[0], held.at[i], in_sem.at[i]).wait()
+            facts[0] = jnp.maximum(sides[0], sides[1])
+            for i, block in enumerate(order_codes(table_ref)):
+                facts[1 + i] = block
+        for i in range(count):
+            for h in range(len(parts)):
+                pltpu.make_async_copy(
+                    refs[0], held.at[i, pl.ds(h * rows, rows)], in_sem.at[i, h]
+                ).wait()
             pltpu.make_async_copy(held.at[i], outs[i], out_sem.at[i]).start()
         for i in range(count):
             pltpu.make_async_copy(held.at[i], outs[i], out_sem.at[i]).wait()
 
     return pl.pallas_call(
         kernel,
-        out_shape=[jax.ShapeDtypeStruct(piece, pools[0].dtype)] * count
-        + [jax.ShapeDtypeStruct((1,), jnp.int32)] * tally,
-        grid_spec=pltpu.PrefetchScalarGridSpec(
-            num_scalar_prefetch=1,
-            grid=(1,),
-            in_specs=[pl.BlockSpec(memory_space=pl.ANY)] * len(pools),
-            out_specs=[pl.BlockSpec(memory_space=pl.ANY)] * count
-            + [pl.BlockSpec(memory_space=pltpu.SMEM)] * tally,
-            scratch_shapes=[
-                pltpu.VMEM((count,) + piece, pools[0].dtype),
-                pltpu.SemaphoreType.DMA((count,)),
-                pltpu.SemaphoreType.DMA((count,)),
-            ],
-        ),
+        out_shape=[jax.ShapeDtypeStruct(piece, kind)] * count
+        + [jax.ShapeDtypeStruct((5,), jnp.int32)] * tally,
+        in_specs=[pl.BlockSpec(memory_space=pltpu.SMEM)]
+        + [pl.BlockSpec(memory_space=pl.ANY)] * len(flat),
+        out_specs=[pl.BlockSpec(memory_space=pl.ANY)] * count
+        + [pl.BlockSpec(memory_space=pltpu.SMEM)] * tally,
+        scratch_shapes=[
+            pltpu.VMEM((count,) + piece, kind),
+            pltpu.SemaphoreType.DMA((count, len(parts))),
+            pltpu.SemaphoreType.DMA((count,)),
+        ],
         cost_estimate=pl.CostEstimate(
             flops=0, transcendentals=0, bytes_accessed=4 * count * piece[0] * piece[1]
         ),
-    )(table, *pools)
+    )(table, *flat)
 
 
 def unwritten(count, shape, dtype):
@@ -204,13 +220,13 @@
 def slot_codes(first):
     def codes(table):
         y, z_lo, core = place()
-        found = [(jnp.int32(0), jnp.int32(0))] * 2
+        found = [jnp.int32(0)] * 2
         rank = jnp.int32(0)
         for k, hit in enumerate(crossing(table, z_lo, 1 - z_lo)):
-            pool, index = (core != k % 2).astype(jnp.int32), (y - k // 2 + 4) % 4
+            pool = 4 * (core != k % 2).astype(jnp.int32) + (y - k // 2 + 4) % 4
             for j in range(2):
                 here = (hit == 1) & (rank == 2 * (first + j) + core)
-                found[j] = jnp.where(here, pool, found[j][0]), jnp.where(here, index, found[j][1])
+                found[j] = jnp.where(here, pool, found[j])
             rank = rank + hit
         return found
 
@@ -227,11 +243,9 @@
         rank = jnp.int32(0)
         for k in range(8):
             rank = rank + jnp.where(k < 2 * tile_y + tile_core, present[k], 0)
-        slot = rank // 2
-        near = tile_z == z_lo
-        other = jnp.where(near, tile_core, rank % 2) != core
-        pool = jnp.where(near, 0, 2 + 2 * slot) + other.astype(jnp.int32)
-        found.append((pool, jnp.where(near, (y - tile_y + 4) % 4, 0)))
+        near = 4 * (tile_core != core).astype(jnp.int32) + (y - tile_y + 4) % 4
+        far = 8 + 2 * (rank // 2) + (rank % 2 != core).astype(jnp.int32)
+        found.append(jnp.where(tile_z == z_lo, near, far))
     return found
 
 
@@ -258,31 +272,41 @@
     strings = coeffs.shape[0]
     rows = 16
     alpha_pieces = coeffs.reshape(rows, strings // rows, strings)
-    beta_pieces = coeffs.reshape(4, strings // 4, strings)
-
-    near = [shift(beta_pieces[s], "y", s) for s in (1, 2, 3)]
-    near = jnp.stack([beta_pieces[0]] + near)
+    beta_pieces = coeffs.reshape(4, 2, strings // 8, strings)
+
+    near = []
+    for h in range(2):
+        near.append([shift(beta_pieces[s, h], "y", s) for s in (1, 2, 3)])
     alpha_held = exchange(alpha_pieces, ("zh", "x"))
 
-    near_twin = swap(near, "core")
-    *slots, most = copy_pieces([near, near_twin], beta_list, 2, slot_codes(0), tally=True)
-    slots = [swap(slot, "zl")[None] for slot in slots]
+    slots = []
+    for h in range(2):
+        near[h] = [beta_pieces[0, h]] + near[h]
+        near[h] = near[h] + [swap(piece, "core") for piece in near[h]]
+        *sent, facts = copy_pieces([near[h]], beta_list, 2, slot_codes(0), tally=True)
+        slots.append([swap(slot, "zl") for slot in sent])
 
     def carry():
-        more = copy_pieces([near, near_twin], beta_list, 2, slot_codes(2))
-        more = [swap(slot, "zl") for slot in more]
-        return tuple(more + [swap(slot, "core") for slot in more])
+        more = []
+        for h in range(2):
+            sent = copy_pieces([near[h]], beta_list, 2, slot_codes(2))
+            sent = [swap(slot, "zl") for slot in sent]
+            more += sent + [swap(slot, "core") for slot in sent]
+        return tuple(more)
 
     def skip():
-        return tuple(unwritten(4, near.shape[1:], near.dtype))
-
-    more = lax.cond(most[0] > 4, carry, skip)
-    pools = [near, near_twin]
-    for slot in slots:
-        pools += [slot, swap(slot, "core")]
-    for own, twin in zip(more[:2], more[2:]):
-        pools += [own[None], twin[None]]
-    leaving = copy_pieces(pools, beta_list, 4, send_codes)
+        return tuple(unwritten(8, near[0][0].shape, near[0][0].dtype))
+
+    more = lax.cond(facts[0] > 4, carry, skip)
+    parts = []
+    for h in range(2):
+        pools = list(near[h])
+        for slot in slots[h]:
+            pools += [slot, swap(slot, "core")]
+        for j in range(2):
+            pools += [more[4 * h + j], more[4 * h + 2 + j]]
+        parts.append(pools)
+    leaving = copy_pieces(parts, beta_list, 4, send_codes)
     arrived = [leaving[0]] + [shift(leaving[s], "y", s) for s in (1, 2, 3)]
 
     alpha_out = gather_pieces(alpha_held, alpha_list)
@@ -291,7 +315,7 @@
     terms, alpha_dense, beta_dense = own_terms(
         coeffs, alpha_blocks, alpha_cols, beta_blocks, beta_cols
     )
-    terms = add_beta(beta_list, terms, arrived, beta_dense)
+    terms = add_beta(facts, terms, arrived, beta_dense)
     return add_alpha(terms, alpha_dense, alpha_fetched)
 
 

time: 190 us -> 191 us (level)
  waiting for transfers between devices: 116 us -> 52.6 us
  blocking collectives: 0 us -> 62.1 us
  starting transfers between devices: 28.6 us -> 24.6 us
  local copies, waits for them, and re-layouts: 4.76 us -> 8.42 us
  Pallas kernels: 37.6 us -> 40.1 us
    all_to_all x0 -> x1, blocking collectives: none -> 62.1 us  [exchange(): return lax.all_to_all(value, axis, split_axis=0, concat_axis=0, tiled=True)]
    all_to_all x2 -> x1, waiting for transfers between devices: 45.4 us -> 0.01 us  [exchange(): return lax.all_to_all(value, axis, split_axis=0, concat_axis=0, tiled=True)]
    ppermute x5 -> x16, waiting for transfers between devices: 62 us -> 27.5 us  [swap(): return lax.ppermute(value, axis, [(0, 1), (1, 0)])]
    ppermute x6 -> x9, waiting for transfers between devices: 8.12 us -> 25.2 us  [shift(): lax.ppermute(value, axis, [(i, (i + step) % count) for i in range(count)])]
    all_to_all x2 -> x1, starting transfers between devices: 14.8 us -> 3.81 us  [exchange(): return lax.all_to_all(value, axis, split_axis=0, concat_axis=0, tiled=True)]
    ppermute x5 -> x16, starting transfers between devices: 2.21 us -> 5.87 us  [swap(): return lax.ppermute(value, axis, [(0, 1), (1, 0)])]
    ppermute x6 -> x9, starting transfers between devices: 11.6 us -> 14.9 us  [shift(): lax.ppermute(value, axis, [(i, (i + step) % count) for i in range(count)])]
    pallas_call x2 -> x3, Pallas kernels: 6.42 us -> 9.55 us  [copy_pieces(): pl.pallas_call(kernel, out_shape=[jax.ShapeDtypeStruct(piece, kind)] * co...]
  transfers between devices with their start and end apart: 13 -> 26, of which waited for: 6 -> 10; matrix products, arithmetic and copies ran while one was open for 2% -> 2% of each run, Pallas kernels for 16% -> 16%
where the time goes in v2:
time: 191 us; the launch traced here: 189 us
  blocking collectives  62.1 us (33%)
  waiting for transfers between devices  52.6 us (28%)
  Pallas kernels  40.1 us (21%)
  starting transfers between devices  24.6 us (13%)
  local copies, waits for them, and re-layouts  8.42 us (4%)
    all_to_all x1, blocking collectives, exchange(): return lax.all_to_all(value, axis, split_axis=0, concat_axis=0, tiled=True)  62.1 us
    ppermute x16, waiting for transfers between devices, swap(): return lax.ppermute(value, axis, [(0, 1), (1, 0)])  27.5 us
    ppermute x9, waiting for transfers between devices, shift(): lax.ppermute(value, axis, [(i, (i + step) % count) for i in range(count)])  25.2 us
    ppermute x9, starting transfers between devices, shift(): lax.ppermute(value, axis, [(i, (i + step) % count) for i in range(count)])  14.9 us
    pallas_call x1, Pallas kernels, own_terms(): pl.pallas_call(kernel, out_shape=[jax.ShapeDtypeStruct(square, jnp.float3...  12.3 us
    pallas_call x3, Pallas kernels, copy_pieces(): pl.pallas_call(kernel, out_shape=[jax.ShapeDtypeStruct(piece, kind)] * co...  9.55 us
    pallas_call x1, Pallas kernels, add_beta(): pl.pallas_call(kernel, out_shape=jax.ShapeDtypeStruct(terms.shape, jnp.fl...  8.07 us
    pallas_call x1, Pallas kernels, add_alpha(): pl.pallas_call(kernel, out_shape=jax.ShapeDtypeStruct(terms.shape, fetche...  6.06 us
  transfers between devices with their start and end apart: 26, of which 10 were waited for; matrix products, arithmetic and copies ran while one was open for 2% of the time, Pallas kernels for 16%

profile of v2, /device:TPU:32, one launch (start us, length us, event | category | flops | bytes accessed | tf_op | source)
XLA Modules:
  0.0 189.0 jit_solution(2269064196899742798)
XLA Ops:
  0.0 62.1 %all_to_all.10.source = bf16[16,64,1024]{2,1,0:T(8,128)(2,1)} all-to-all(bf16[16,64,1024]{2,1,0:T(8,128)(2,1)} %bitcast.22), channel_id=1, replica_groups=mesh['zh'=4,'x'=4,'y'=4,'zl'=2,'core'=2] {'zh','x'}, dimensions={0} | all-to-all | bytes 4194304 | tf_op jit(solution)/shard_map/all_to_all | solution.py:263
  62.1 4.2 %shard_map.78 = bf16[16,64,1024]{2,1,0:T(8,128)(2,1)} custom-call(s32[16]{0:T(128)} %table_ref.7, bf16[16,64,1024]{2,1,0:T(8,128)(2,1)} %all_to_all.10.source), custom_call_target="tpu_custom_call" | custom-call | bytes 4194304 | tf_op jit(solution)/shard_map/pallas_call | solution.py:187
  66.3 3.8 %all-to-all-start.1 = ((bf16[16,64,1024]{2,1,0:T(8,128)(2,1)}), bf16[16,64,1024]{2,1,0:T(8,128)(2,1)S(1)}, u32[]{:S(2)}, u32[]{:S(2)}) async-start(bf16[16,64,1024]{2,1,0:T(8,128)(2,1)} %shard_map.78), calls=%async_computation.1 | async-start | bytes 4194304 | tf_op jit(solution)/shard_map/all_to_all | solution.py:263
  70.1 1.7 slice_bitcast_fusion
  71.9 1.7 collective-permute-start.8
  73.5 2.9 %collective-permute-start.9 = (bf16[128,1024]{1,0:T(8,128)(2,1)S(1)}, bf16[128,1024]{1,0:T(8,128)(2,1)S(1)}, u32[]{:S(2)}, u32[]{:S(2)}) collective-permute-start(bf16[128,1024]{1,0:T(8,128)(2,1)S(1)} %get-tuple-element.105), channel_id=1, source_target_pairs={{0,8},{4,12},{8,0},{12,4},{1,9},{5,13},{9,1},{13,5},{2,10},{6,14},... | collective-permute-start | bytes 786440 | tf_op jit(solution)/shard_map/ppermute | solution.py:268
  79.3 3.4 %collective-permute-done.8.refs_1_.refs_17_ = bf16[128,1024]{1,0:T(8,128)(2,1)S(1)} collective-permute-done((bf16[128,1024]{1,0:T(8,128)(2,1)S(1)}, bf16[128,1024]{1,0:T(8,128)(2,1)S(1)}, u32[]{:S(2)}, u32[]{:S(2)}) %collective-permute-start.8) | collective-permute-done | bytes 262176 | tf_op jit(solution)/shard_map/ppermute | solution.py:268
  82.6 1.5 collective-permute-start.17
  84.2 5.1 %collective-permute-done.9.refs_2_.refs_18_ = bf16[128,1024]{1,0:T(8,128)(2,1)S(1)} collective-permute-done((bf16[128,1024]{1,0:T(8,128)(2,1)S(1)}, bf16[128,1024]{1,0:T(8,128)(2,1)S(1)}, u32[]{:S(2)}, u32[]{:S(2)}) %collective-permute-start.9) | collective-permute-done | bytes 262176 | tf_op jit(solution)/shard_map/ppermute | solution.py:268
  89.8 2.8 %collective-permute-done.15.refs_1_ = bf16[128,1024]{1,0:T(8,128)(2,1)} collective-permute-done((bf16[128,1024]{1,0:T(8,128)(2,1)S(1)}, bf16[128,1024]{1,0:T(8,128)(2,1)}, u32[]{:S(2)}, u32[]{:S(2)}) %collective-permute-start.15) | collective-permute-done | bytes 262176 | tf_op jit(solution)/shard_map/ppermute | solution.py:268
  92.5 6.3 %collective-permute-done.16.refs_2_ = bf16[128,1024]{1,0:T(8,128)(2,1)} collective-permute-done((bf16[128,1024]{1,0:T(8,128)(2,1)S(1)}, bf16[128,1024]{1,0:T(8,128)(2,1)}, u32[]{:S(2)}, u32[]{:S(2)}) %collective-permute-start.16) | collective-permute-done | bytes 262176 | tf_op jit(solution)/shard_map/ppermute | solution.py:268
  100.7 3.0 %shard_map.73 = (bf16[128,1024]{1,0:T(8,128)(2,1)}, bf16[128,1024]{1,0:T(8,128)(2,1)}, s32[5]{0:T(128)}) custom-call(s32[16]{0:T(128)S(1)} %copy-done.16, bf16[128,1024]{1,0:T(8,128)(2,1)S(1)} %get-tuple-element.107.refs_0_.refs_16_, bf16[128,1024]{1,0:T(8,128)(2,1)S(1)} %collective-permute-done.8.refs_1_.refs_17_, ...), custom_call_target="tpu_custom_call" | custom-call | bytes 1048576 | tf_op jit(solution)/shard_map/pallas_call | solution.py:148
  106.9 2.9 %shard_map.75 = (bf16[128,1024]{1,0:T(8,128)(2,1)}, bf16[128,1024]{1,0:T(8,128)(2,1)}, s32[5]{0:T(128)}) custom-call(s32[16]{0:T(128)S(1)} %copy-done.16, bf16[128,1024]{1,0:T(8,128)(2,1)S(1)} %get-tuple-element.103.refs_0_, bf16[128,1024]{1,0:T(8,128)(2,1)} %collective-permute-done.15.refs_1_, bf16[128,1024]{1,0:T(8,128)(2,1)} %collective-permute-done.16.refs_2_, ...), custom_call_target="tpu_custom_call" | custom-call | bytes 1048576 | tf_op jit(solution)/shard_map/pallas_call | solution.py:148
  111.9 12.0 %collective-permute-done.26.refs_24_ = bf16[128,1024]{1,0:T(8,128)(2,1)} collective-permute-done((bf16[128,1024]{1,0:T(8,128)(2,1)}, bf16[128,1024]{1,0:T(8,128)(2,1)}, u32[]{:S(2)}, u32[]{:S(2)}) %collective-permute-start.26) | collective-permute-done | bytes 262176 | tf_op jit(solution)/shard_map/ppermute | solution.py:259
  123.9 5.6 %collective-permute-done.28.refs_26_ = bf16[128,1024]{1,0:T(8,128)(2,1)} collective-permute-done((bf16[128,1024]{1,0:T(8,128)(2,1)}, bf16[128,1024]{1,0:T(8,128)(2,1)}, u32[]{:S(2)}, u32[]{:S(2)}) %collective-permute-start.28) | collective-permute-done | bytes 262176 | tf_op jit(solution)/shard_map/ppermute | solution.py:259
  129.5 5.5 %collective-permute-done.22.refs_8_ = bf16[128,1024]{1,0:T(8,128)(2,1)S(1)} collective-permute-done((bf16[128,1024]{1,0:T(8,128)(2,1)}, bf16[128,1024]{1,0:T(8,128)(2,1)S(1)}, u32[]{:S(2)}, u32[]{:S(2)}) %collective-permute-start.22) | collective-permute-done | bytes 262176 | tf_op jit(solution)/shard_map/ppermute | solution.py:259
  135.7 3.5 %collective-permute-done.24.refs_10_ = bf16[128,1024]{1,0:T(8,128)(2,1)S(1)} collective-permute-done((bf16[128,1024]{1,0:T(8,128)(2,1)}, bf16[128,1024]{1,0:T(8,128)(2,1)S(1)}, u32[]{:S(2)}, u32[]{:S(2)}) %collective-permute-start.24) | collective-permute-done | bytes 262176 | tf_op jit(solution)/shard_map/ppermute | solution.py:259
  141.5 3.6 %shard_map.76 = (bf16[256,1024]{1,0:T(8,128)(2,1)}, bf16[256,1024]{1,0:T(8,128)(2,1)}, bf16[256,1024]{1,0:T(8,128)(2,1)}, bf16[256,1024]{1,0:T(8,128)(2,1)}) custom-call(s32[16]{0:T(128)S(1)} %copy-done.16, bf16[128,1024]{1,0:T(8,128)(2,1)S(1)} %get-tuple-element.103.refs_0_, bf16[128,1024]{1,0:T(8,128)(2,1)} %collective-permute-done.15.refs_1_, ...), custom_call_target="tpu_custom_call" | custom-call | bytes 4194304 | tf_op jit(solution)/shard_map/pallas_call | solution.py:148
  145.2 1.8 collective-permute-start.30
  147.0 2.8 %collective-permute-start.31 = (bf16[256,1024]{1,0:T(8,128)(2,1)}, bf16[256,1024]{1,0:T(8,128)(2,1)S(1)}, u32[]{:S(2)}, u32[]{:S(2)}) collective-permute-start(bf16[256,1024]{1,0:T(8,128)(2,1)} %get-tuple-element.97), channel_id=1, source_target_pairs={{0,8},{4,12},{8,0},{12,4},{1,9},{5,13},{9,1},{13,5},{2,10},{6,14},... | collective-permute-start | bytes 1572872 | tf_op jit(solution)/shard_map/ppermute | solution.py:268
  152.8 12.3 %shard_map.74 = (f32[1024,1024]{1,0:T(8,128)}, bf16[1024,1024]{1,0:T(8,128)(2,1)}, bf16[1024,1024]{1,0:T(8,128)(2,1)}) custom-call(s32[80]{0:T(128)} %reshape.20.a_table, s32[80]{0:T(128)} %reshape.21.b_table, bf16[1024,1024]{1,0:T(8,128)(2,1)} %c.1, bf16[8,2,5,128,128]{4,3,2,1,0:T(8,128)(2,1)} %a_blocks.1, bf16[8,2,5,128,128]{4,3,2,1,0:T(8,128)(2,1)} %b_blocks.1), custom_call_target="tpu_custom_call" | custom-call | flops 4294967296 | bytes 15728640 | tf_op jit(solution)/shard_map/pallas_call | solution.py:43
  165.0 7.7 %collective-permute-done.31.refs_2_ = bf16[256,1024]{1,0:T(8,128)(2,1)S(1)} collective-permute-done((bf16[256,1024]{1,0:T(8,128)(2,1)}, bf16[256,1024]{1,0:T(8,128)(2,1)S(1)}, u32[]{:S(2)}, u32[]{:S(2)}) %collective-permute-start.31) | collective-permute-done | bytes 524320 | tf_op jit(solution)/shard_map/ppermute | solution.py:268
  173.5 8.1 %shard_map.77.terms_ref = f32[1024,1024]{1,0:T(8,128)} custom-call(s32[5]{0:T(128)} %get-tuple-element.80.facts_ref, f32[1024,1024]{1,0:T(8,128)} %get-tuple-element.81.terms_ref, bf16[1024,1024]{1,0:T(8,128)(2,1)} %get-tuple-element.82.dense_ref, bf16[256,1024]{1,0:T(8,128)(2,1)} %get-tuple-element.95.refs_0_, ...), custom_call_target="tpu_custom_call", output_to_operand_aliasing={{}: (1, {})} | custom-call | flops 2147483648 | bytes 12582912 | tf_op jit(solution)/shard_map/pallas_call | solution.py:74
  183.0 6.1 %shard_map.79 = bf16[1024,1024]{1,0:T(8,128)(2,1)} custom-call(f32[1024,1024]{1,0:T(8,128)} %shard_map.77.terms_ref, bf16[1024,1024]{1,0:T(8,128)(2,1)} %get-tuple-element.99.dense_ref, bf16[1024,1024]{1,0:T(8,128)(2,1)} %bitcast.21), custom_call_target="tpu_custom_call" | custom-call | flops 2147483648 | bytes 10485760 | tf_op jit(solution)/shard_map/pallas_call | solution.py:100
  (73 shorter events, 17.9 us)
Async XLA Ops:
  66.3 115.3 %all-to-all-start.1 = ((bf16[16,64,1024]{2,1,0:T(8,128)(2,1)}), bf16[16,64,1024]{2,1,0:T(8,128)(2,1)S(1)}, u32[]{:S(2)}, u32[]{:S(2)}) async-start(bf16[16,64,1024]{2,1,0:T(8,128)(2,1)} %shard_map.78), calls=%async_computation.1 | async-start | bytes 4194304 | tf_op jit(solution)/shard_map/all_to_all | solution.py:263
  71.9 10.7 %collective-permute-start.8 = (bf16[128,1024]{1,0:T(8,128)(2,1)S(1)}, bf16[128,1024]{1,0:T(8,128)(2,1)S(1)}, u32[]{:S(2)}, u32[]{:S(2)}) collective-permute-start(bf16[128,1024]{1,0:T(8,128)(2,1)S(1)} %get-tuple-element.106), channel_id=1, source_target_pairs={{0,4},{4,8},{8,12},{12,0},{1,5},{5,9},{9,13},{13,1},{2,6},{6,10},{... | collective-permute-start | bytes 786440 | tf_op jit(solution)/shard_map/ppermute | solution.py:268
  73.5 15.7 %collective-permute-start.9 = (bf16[128,1024]{1,0:T(8,128)(2,1)S(1)}, bf16[128,1024]{1,0:T(8,128)(2,1)S(1)}, u32[]{:S(2)}, u32[]{:S(2)}) collective-permute-start(bf16[128,1024]{1,0:T(8,128)(2,1)S(1)} %get-tuple-element.105), channel_id=1, source_target_pairs={{0,8},{4,12},{8,0},{12,4},{1,9},{5,13},{9,1},{13,5},{2,10},{6,14},... | collective-permute-start | bytes 786440 | tf_op jit(solution)/shard_map/ppermute | solution.py:268
  76.4 12.8 %collective-permute-start.10 = (bf16[128,1024]{1,0:T(8,128)(2,1)S(1)}, bf16[128,1024]{1,0:T(8,128)(2,1)S(1)}, u32[]{:S(2)}, u32[]{:S(2)}) collective-permute-start(bf16[128,1024]{1,0:T(8,128)(2,1)S(1)} %get-tuple-element.104), channel_id=1, source_target_pairs={{0,12},{4,0},{8,4},{12,8},{1,13},{5,1},{9,5},{13,9},{2,14},{6,2},{... | collective-permute-start | bytes 786440 | tf_op jit(solution)/shard_map/ppermute | solution.py:268
  77.8 14.7 %collective-permute-start.15 = (bf16[128,1024]{1,0:T(8,128)(2,1)S(1)}, bf16[128,1024]{1,0:T(8,128)(2,1)}, u32[]{:S(2)}, u32[]{:S(2)}) collective-permute-start(bf16[128,1024]{1,0:T(8,128)(2,1)S(1)} %get-tuple-element.102), channel_id=1, source_target_pairs={{0,4},{4,8},{8,12},{12,0},{1,5},{5,9},{9,13},{13,1},{2,6},{6,10},{... | collective-permute-start | bytes 786440 | tf_op jit(solution)/shard_map/ppermute | solution.py:268
  78.5 20.4 %collective-permute-start.16 = (bf16[128,1024]{1,0:T(8,128)(2,1)S(1)}, bf16[128,1024]{1,0:T(8,128)(2,1)}, u32[]{:S(2)}, u32[]{:S(2)}) collective-permute-start(bf16[128,1024]{1,0:T(8,128)(2,1)S(1)} %get-tuple-element.101), channel_id=1, source_target_pairs={{0,8},{4,12},{8,0},{12,4},{1,9},{5,13},{9,1},{13,5},{2,10},{6,14},... | collective-permute-start | bytes 786440 | tf_op jit(solution)/shard_map/ppermute | solution.py:268
  82.6 16.2 %collective-permute-start.17 = (bf16[128,1024]{1,0:T(8,128)(2,1)S(1)}, bf16[128,1024]{1,0:T(8,128)(2,1)}, u32[]{:S(2)}, u32[]{:S(2)}) collective-permute-start(bf16[128,1024]{1,0:T(8,128)(2,1)S(1)} %get-tuple-element.100), channel_id=1, source_target_pairs={{0,12},{4,0},{8,4},{12,8},{1,13},{5,1},{9,5},{13,9},{2,14},{6,2},{... | collective-permute-start | bytes 786440 | tf_op jit(solution)/shard_map/ppermute | solution.py:268
  89.3 10.1 %collective-permute-start.11 = (bf16[128,1024]{1,0:T(8,128)(2,1)S(1)}, bf16[128,1024]{1,0:T(8,128)(2,1)S(1)}, u32[]{:S(2)}, u32[]{:S(2)}) collective-permute-start(bf16[128,1024]{1,0:T(8,128)(2,1)S(1)} %get-tuple-element.107.refs_0_.refs_16_), channel_id=1, source_target_pairs={{0,1},{1,0},{2,3},{3,2},{4,5},{5,4},{6,7},{7,6},{8,9},{9,8},{10,11... | collective-permute-start | bytes 786440 | tf_op jit(solution)/shard_map/ppermute | solution.py:259
  89.3 10.2 %collective-permute-start.12 = (bf16[128,1024]{1,0:T(8,128)(2,1)S(1)}, bf16[128,1024]{1,0:T(8,128)(2,1)S(1)}, u32[]{:S(2)}, u32[]{:S(2)}) collective-permute-start(bf16[128,1024]{1,0:T(8,128)(2,1)S(1)} %collective-permute-done.8.refs_1_.refs_17_), channel_id=1, source_target_pairs={{0,1},{1,0},{2,3},{3,2},{4,5},{5,4},{6,7},{7,6},{8,9},{9,8},{10,11... | collective-permute-start | bytes 786440 | tf_op jit(solution)/shard_map/ppermute | solution.py:259
  92.5 7.3 %collective-permute-start.13 = (bf16[128,1024]{1,0:T(8,128)(2,1)S(1)}, bf16[128,1024]{1,0:T(8,128)(2,1)S(1)}, u32[]{:S(2)}, u32[]{:S(2)}) collective-permute-start(bf16[128,1024]{1,0:T(8,128)(2,1)S(1)} %collective-permute-done.9.refs_2_.refs_18_), channel_id=1, source_target_pairs={{0,1},{1,0},{2,3},{3,2},{4,5},{5,4},{6,7},{7,6},{8,9},{9,8},{10,11... | collective-permute-start | bytes 786440 | tf_op jit(solution)/shard_map/ppermute | solution.py:259
  98.8 7.0 %collective-permute-start.18 = (bf16[128,1024]{1,0:T(8,128)(2,1)S(1)}, bf16[128,1024]{1,0:T(8,128)(2,1)}, u32[]{:S(2)}, u32[]{:S(2)}) collective-permute-start(bf16[128,1024]{1,0:T(8,128)(2,1)S(1)} %get-tuple-element.103.refs_0_), channel_id=1, source_target_pairs={{0,1},{1,0},{2,3},{3,2},{4,5},{5,4},{6,7},{7,6},{8,9},{9,8},{10,11... | collective-permute-start | bytes 786440 | tf_op jit(solution)/shard_map/ppermute | solution.py:259
  99.3 6.5 %collective-permute-start.19 = (bf16[128,1024]{1,0:T(8,128)(2,1)}, bf16[128,1024]{1,0:T(8,128)(2,1)}, u32[]{:S(2)}, u32[]{:S(2)}) collective-permute-start(bf16[128,1024]{1,0:T(8,128)(2,1)} %collective-permute-done.15.refs_1_), channel_id=1, source_target_pairs={{0,1},{1,0},{2,3},{3,2},{4,5},{5,4},{6,7},{7,6},{8,9},{9,8},{10,11... | collective-permute-start | bytes 786440 | tf_op jit(solution)/shard_map/ppermute | solution.py:259
  99.5 6.4 %collective-permute-start.20 = (bf16[128,1024]{1,0:T(8,128)(2,1)}, bf16[128,1024]{1,0:T(8,128)(2,1)}, u32[]{:S(2)}, u32[]{:S(2)}) collective-permute-start(bf16[128,1024]{1,0:T(8,128)(2,1)} %collective-permute-done.16.refs_2_), channel_id=1, source_target_pairs={{0,1},{1,0},{2,3},{3,2},{4,5},{5,4},{6,7},{7,6},{8,9},{9,8},{10,11... | collective-permute-start | bytes 786440 | tf_op jit(solution)/shard_map/ppermute | solution.py:259
  100.0 5.8 %collective-permute-start.21 = (bf16[128,1024]{1,0:T(8,128)(2,1)}, bf16[128,1024]{1,0:T(8,128)(2,1)}, u32[]{:S(2)}, u32[]{:S(2)}) collective-permute-start(bf16[128,1024]{1,0:T(8,128)(2,1)} %collective-permute-done.17.refs_3_), channel_id=1, source_target_pairs={{0,1},{1,0},{2,3},{3,2},{4,5},{5,4},{6,7},{7,6},{8,9},{9,8},{10,11... | collective-permute-start | bytes 786440 | tf_op jit(solution)/shard_map/ppermute | solution.py:259
  104.4 19.5 %collective-permute-start.26 = (bf16[128,1024]{1,0:T(8,128)(2,1)}, bf16[128,1024]{1,0:T(8,128)(2,1)}, u32[]{:S(2)}, u32[]{:S(2)}) collective-permute-start(bf16[128,1024]{1,0:T(8,128)(2,1)} %get-tuple-element.89), channel_id=1, source_target_pairs={{0,2},{2,0},{1,3},{3,1},{4,6},{6,4},{5,7},{7,5},{8,10},{10,8},{9,1... | collective-permute-start | bytes 786440 | tf_op jit(solution)/shard_map/ppermute | solution.py:259
  106.1 23.4 %collective-permute-start.28 = (bf16[128,1024]{1,0:T(8,128)(2,1)}, bf16[128,1024]{1,0:T(8,128)(2,1)}, u32[]{:S(2)}, u32[]{:S(2)}) collective-permute-start(bf16[128,1024]{1,0:T(8,128)(2,1)} %get-tuple-element.90), channel_id=1, source_target_pairs={{0,2},{2,0},{1,3},{3,1},{4,6},{6,4},{5,7},{7,5},{8,10},{10,8},{9,1... | collective-permute-start | bytes 786440 | tf_op jit(solution)/shard_map/ppermute | solution.py:259
  109.8 25.2 %collective-permute-start.22 = (bf16[128,1024]{1,0:T(8,128)(2,1)}, bf16[128,1024]{1,0:T(8,128)(2,1)S(1)}, u32[]{:S(2)}, u32[]{:S(2)}) collective-permute-start(bf16[128,1024]{1,0:T(8,128)(2,1)} %get-tuple-element.83), channel_id=1, source_target_pairs={{0,2},{2,0},{1,3},{3,1},{4,6},{6,4},{5,7},{7,5},{8,10},{10,8},{9,1... | collective-permute-start | bytes 786440 | tf_op jit(solution)/shard_map/ppermute | solution.py:259
  111.3 27.9 %collective-permute-start.24 = (bf16[128,1024]{1,0:T(8,128)(2,1)}, bf16[128,1024]{1,0:T(8,128)(2,1)S(1)}, u32[]{:S(2)}, u32[]{:S(2)}) collective-permute-start(bf16[128,1024]{1,0:T(8,128)(2,1)} %get-tuple-element.84), channel_id=1, source_target_pairs={{0,2},{2,0},{1,3},{3,1},{4,6},{6,4},{5,7},{7,5},{8,10},{10,8},{9,1... | collective-permute-start | bytes 786440 | tf_op jit(solution)/shard_map/ppermute | solution.py:259
  123.9 15.3 %collective-permute-start.27 = (bf16[128,1024]{1,0:T(8,128)(2,1)}, bf16[128,1024]{1,0:T(8,128)(2,1)S(1)}, u32[]{:S(2)}, u32[]{:S(2)}) collective-permute-start(bf16[128,1024]{1,0:T(8,128)(2,1)} %collective-permute-done.26.refs_24_), channel_id=1, source_target_pairs={{0,1},{1,0},{2,3},{3,2},{4,5},{5,4},{6,7},{7,6},{8,9},{9,8},{10,11... | collective-permute-start | bytes 786440 | tf_op jit(solution)/shard_map/ppermute | solution.py:259
  129.5 9.7 %collective-permute-start.29 = (bf16[128,1024]{1,0:T(8,128)(2,1)}, bf16[128,1024]{1,0:T(8,128)(2,1)S(1)}, u32[]{:S(2)}, u32[]{:S(2)}) collective-permute-start(bf16[128,1024]{1,0:T(8,128)(2,1)} %collective-permute-done.28.refs_26_), channel_id=1, source_target_pairs={{0,1},{1,0},{2,3},{3,2},{4,5},{5,4},{6,7},{7,6},{8,9},{9,8},{10,11... | collective-permute-start | bytes 786440 | tf_op jit(solution)/shard_map/ppermute | solution.py:259
  135.7 3.5 %collective-permute-start.23 = (bf16[128,1024]{1,0:T(8,128)(2,1)S(1)}, bf16[128,1024]{1,0:T(8,128)(2,1)S(1)}, u32[]{:S(2)}, u32[]{:S(2)}) collective-permute-start(bf16[128,1024]{1,0:T(8,128)(2,1)S(1)} %collective-permute-done.22.refs_8_), channel_id=1, source_target_pairs={{0,1},{1,0},{2,3},{3,2},{4,5},{5,4},{6,7},{7,6},{8,9},{9,8},{10,11... | collective-permute-start | bytes 786440 | tf_op jit(solution)/shard_map/ppermute | solution.py:259
  145.2 19.9 %collective-permute-start.30 = (bf16[256,1024]{1,0:T(8,128)(2,1)}, bf16[256,1024]{1,0:T(8,128)(2,1)S(1)}, u32[]{:S(2)}, u32[]{:S(2)}) collective-permute-start(bf16[256,1024]{1,0:T(8,128)(2,1)} %get-tuple-element.96), channel_id=1, source_target_pairs={{0,4},{4,8},{8,12},{12,0},{1,5},{5,9},{9,13},{13,1},{2,6},{6,10},{... | collective-permute-start | bytes 1572872 | tf_op jit(solution)/shard_map/ppermute | solution.py:268
  147.0 25.7 %collective-permute-start.31 = (bf16[256,1024]{1,0:T(8,128)(2,1)}, bf16[256,1024]{1,0:T(8,128)(2,1)S(1)}, u32[]{:S(2)}, u32[]{:S(2)}) collective-permute-start(bf16[256,1024]{1,0:T(8,128)(2,1)} %get-tuple-element.97), channel_id=1, source_target_pairs={{0,8},{4,12},{8,0},{12,4},{1,9},{5,13},{9,1},{13,5},{2,10},{6,14},... | collective-permute-start | bytes 1572872 | tf_op jit(solution)/shard_map/ppermute | solution.py:268
  149.8 22.9 %collective-permute-start.32 = (bf16[256,1024]{1,0:T(8,128)(2,1)}, bf16[256,1024]{1,0:T(8,128)(2,1)}, u32[]{:S(2)}, u32[]{:S(2)}) collective-permute-start(bf16[256,1024]{1,0:T(8,128)(2,1)} %get-tuple-element.98), channel_id=1, source_target_pairs={{0,12},{4,0},{8,4},{12,8},{1,13},{5,1},{9,5},{13,9},{2,14},{6,2},{... | collective-permute-start | bytes 1572872 | tf_op jit(solution)/shard_map/ppermute | solution.py:268
  (17 other events, 72.2 us)

commit v3 on v2

--- a/solution.py
+++ b/solution.py
@@ -56,7 +56,7 @@
     )(alpha_cols.reshape(-1), beta_cols.reshape(-1), coeffs, alpha_blocks, beta_blocks)
 
 
-def add_beta(facts, terms, pieces, dense):
+def add_beta(facts, terms, pieces, dense, first):
     step, size = pieces[0].shape
 
     def kernel(facts_ref, terms_ref, dense_ref, *refs):
@@ -69,7 +69,7 @@
                     piece[...], dense_ref[...], preferred_element_type=jnp.float32
                 )
 
-    rows = pl.BlockSpec((step, size), lambda i, facts: (facts[1 + i], 0))
+    rows = pl.BlockSpec((step, size), lambda i, facts: (facts[1 + first + i], 0))
     piece = pl.BlockSpec((step, size), lambda i, facts: (0, 0))
     return pl.pallas_call(
         kernel,
@@ -83,7 +83,9 @@
         ),
         input_output_aliases={1: 0},
         cost_estimate=pl.CostEstimate(
-            flops=2 * size**3, transcendentals=0, bytes_accessed=12 * size * size
+            flops=2 * len(pieces) * step * size * size,
+            transcendentals=0,
+            bytes_accessed=12 * len(pieces) * step * size,
         ),
     )(facts, terms, dense, *pieces)
 
@@ -307,7 +309,9 @@
             pools += [more[4 * h + j], more[4 * h + 2 + j]]
         parts.append(pools)
     leaving = copy_pieces(parts, beta_list, 4, send_codes)
-    arrived = [leaving[0]] + [shift(leaving[s], "y", s) for s in (1, 2, 3)]
+    beside = shift(leaving[1], "y", 1)
+    late = [shift(leaving[2], "y", 2)]
+    late.append(shift(leaving[3], "y", 3))
 
     alpha_out = gather_pieces(alpha_held, alpha_list)
     alpha_fetched = exchange(alpha_out, ("zh", "x")).reshape(strings, strings)
@@ -315,7 +319,8 @@
     terms, alpha_dense, beta_dense = own_terms(
         coeffs, alpha_blocks, alpha_cols, beta_blocks, beta_cols
     )
-    terms = add_beta(facts, terms, arrived, beta_dense)
+    terms = add_beta(facts, terms, [leaving[0], beside], beta_dense, 0)
+    terms = add_beta(facts, terms, late, beta_dense, 2)
     return add_alpha(terms, alpha_dense, alpha_fetched)
 
 

time: 191 us -> 191 us (level)
  the two profiles are of different devices: /device:TPU:32 before, /device:TPU:50 now
where the time goes in v3:
time: 191 us; the launch traced here: 190 us
  blocking collectives  61.2 us (32%)
  waiting for transfers between devices  56.3 us (29%)
  Pallas kernels  42.8 us (22%)
  starting transfers between devices  20.5 us (11%)
  local copies, waits for them, and re-layouts  8.57 us (4%)
    all_to_all x1, blocking collectives, exchange(): return lax.all_to_all(value, axis, split_axis=0, concat_axis=0, tiled=True)  61.2 us
    ppermute x16, waiting for transfers between devices, swap(): return lax.ppermute(value, axis, [(0, 1), (1, 0)])  28.8 us
    ppermute x9, waiting for transfers between devices, shift(): lax.ppermute(value, axis, [(i, (i + step) % count) for i in range(count)])  27.5 us
    pallas_call x1, Pallas kernels, own_terms(): pl.pallas_call(kernel, out_shape=[jax.ShapeDtypeStruct(square, jnp.float3...  12.3 us
    pallas_call x2, Pallas kernels, add_beta(): pl.pallas_call(kernel, out_shape=jax.ShapeDtypeStruct(terms.shape, jnp.fl...  10.6 us
    ppermute x9, starting transfers between devices, shift(): lax.ppermute(value, axis, [(i, (i + step) % count) for i in range(count)])  9.89 us
    pallas_call x3, Pallas kernels, copy_pieces(): pl.pallas_call(kernel, out_shape=[jax.ShapeDtypeStruct(piece, kind)] * co...  9.63 us
    pallas_call x1, Pallas kernels, add_alpha(): pl.pallas_call(kernel, out_shape=jax.ShapeDtypeStruct(terms.shape, fetche...  6.05 us
  transfers between devices with their start and end apart: 26, of which 11 were waited for; matrix products, arithmetic and copies ran while one was open for 2% of the time, Pallas kernels for 17%

profile of v3, /device:TPU:50, one launch (start us, length us, event | category | flops | bytes accessed | tf_op | source)
XLA Modules:
  0.0 190.5 jit_solution(2891713978089639368)
XLA Ops:
  0.0 61.2 %all_to_all.10.source = bf16[16,64,1024]{2,1,0:T(8,128)(2,1)} all-to-all(bf16[16,64,1024]{2,1,0:T(8,128)(2,1)} %bitcast.22), channel_id=1, replica_groups=mesh['zh'=4,'x'=4,'y'=4,'zl'=2,'core'=2] {'zh','x'}, dimensions={0} | all-to-all | bytes 4194304 | tf_op jit(solution)/shard_map/all_to_all | solution.py:265
  61.2 4.2 %shard_map.79 = bf16[16,64,1024]{2,1,0:T(8,128)(2,1)} custom-call(s32[16]{0:T(128)} %table_ref.7, bf16[16,64,1024]{2,1,0:T(8,128)(2,1)} %all_to_all.10.source), custom_call_target="tpu_custom_call" | custom-call | bytes 4194304 | tf_op jit(solution)/shard_map/pallas_call | solution.py:189
  65.4 5.2 %all-to-all-start.1 = ((bf16[16,64,1024]{2,1,0:T(8,128)(2,1)}), bf16[16,64,1024]{2,1,0:T(8,128)(2,1)S(1)}, u32[]{:S(2)}, u32[]{:S(2)}) async-start(bf16[16,64,1024]{2,1,0:T(8,128)(2,1)} %shard_map.79), calls=%async_computation.1 | async-start | bytes 4194304 | tf_op jit(solution)/shard_map/all_to_all | solution.py:265
  70.6 1.7 slice_bitcast_fusion
  76.5 2.7 %collective-permute-start.16 = (bf16[128,1024]{1,0:T(8,128)(2,1)S(1)}, bf16[128,1024]{1,0:T(8,128)(2,1)}, u32[]{:S(2)}, u32[]{:S(2)}) collective-permute-start(bf16[128,1024]{1,0:T(8,128)(2,1)S(1)} %get-tuple-element.101), channel_id=1, source_target_pairs={{0,8},{4,12},{8,0},{12,4},{1,9},{5,13},{9,1},{13,5},{2,10},{6,14},... | collective-permute-start | bytes 786440 | tf_op jit(solution)/shard_map/ppermute | solution.py:270
  79.2 8.0 %collective-permute-done.8.refs_1_.refs_17_ = bf16[128,1024]{1,0:T(8,128)(2,1)S(1)} collective-permute-done((bf16[128,1024]{1,0:T(8,128)(2,1)S(1)}, bf16[128,1024]{1,0:T(8,128)(2,1)S(1)}, u32[]{:S(2)}, u32[]{:S(2)}) %collective-permute-start.8) | collective-permute-done | bytes 262176 | tf_op jit(solution)/shard_map/ppermute | solution.py:270
  87.2 2.1 %collective-permute-done.10.refs_3_.refs_19_ = bf16[128,1024]{1,0:T(8,128)(2,1)S(1)} collective-permute-done((bf16[128,1024]{1,0:T(8,128)(2,1)S(1)}, bf16[128,1024]{1,0:T(8,128)(2,1)S(1)}, u32[]{:S(2)}, u32[]{:S(2)}) %collective-permute-start.10) | collective-permute-done | bytes 262176 | tf_op jit(solution)/shard_map/ppermute | solution.py:270
  89.3 3.7 %collective-permute-done.15.refs_1_ = bf16[128,1024]{1,0:T(8,128)(2,1)} collective-permute-done((bf16[128,1024]{1,0:T(8,128)(2,1)S(1)}, bf16[128,1024]{1,0:T(8,128)(2,1)}, u32[]{:S(2)}, u32[]{:S(2)}) %collective-permute-start.15) | collective-permute-done | bytes 262176 | tf_op jit(solution)/shard_map/ppermute | solution.py:270
  92.9 3.4 %collective-permute-done.16.refs_2_ = bf16[128,1024]{1,0:T(8,128)(2,1)} collective-permute-done((bf16[128,1024]{1,0:T(8,128)(2,1)S(1)}, bf16[128,1024]{1,0:T(8,128)(2,1)}, u32[]{:S(2)}, u32[]{:S(2)}) %collective-permute-start.16) | collective-permute-done | bytes 262176 | tf_op jit(solution)/shard_map/ppermute | solution.py:270
  96.4 1.8 collective-permute-done.17.refs_3_
  99.6 3.0 %shard_map.73 = (bf16[128,1024]{1,0:T(8,128)(2,1)}, bf16[128,1024]{1,0:T(8,128)(2,1)}, s32[5]{0:T(128)}) custom-call(s32[16]{0:T(128)S(1)} %copy-done.16, bf16[128,1024]{1,0:T(8,128)(2,1)S(1)} %get-tuple-element.107.refs_0_.refs_16_, bf16[128,1024]{1,0:T(8,128)(2,1)S(1)} %collective-permute-done.8.refs_1_.refs_17_, ...), custom_call_target="tpu_custom_call" | custom-call | bytes 1048576 | tf_op jit(solution)/shard_map/pallas_call | solution.py:150
  103.2 1.6 collective-permute-start.26
  105.7 2.9 %shard_map.75 = (bf16[128,1024]{1,0:T(8,128)(2,1)}, bf16[128,1024]{1,0:T(8,128)(2,1)}, s32[5]{0:T(128)}) custom-call(s32[16]{0:T(128)S(1)} %copy-done.16, bf16[128,1024]{1,0:T(8,128)(2,1)S(1)} %get-tuple-element.103.refs_0_, bf16[128,1024]{1,0:T(8,128)(2,1)} %collective-permute-done.15.refs_1_, bf16[128,1024]{1,0:T(8,128)(2,1)} %collective-permute-done.16.refs_2_, ...), custom_call_target="tpu_custom_call" | custom-call | bytes 1048576 | tf_op jit(solution)/shard_map/pallas_call | solution.py:150
  108.7 1.6 collective-permute-start.22
  110.8 13.6 %collective-permute-done.26.refs_24_ = bf16[128,1024]{1,0:T(8,128)(2,1)} collective-permute-done((bf16[128,1024]{1,0:T(8,128)(2,1)}, bf16[128,1024]{1,0:T(8,128)(2,1)}, u32[]{:S(2)}, u32[]{:S(2)}) %collective-permute-start.26) | collective-permute-done | bytes 262176 | tf_op jit(solution)/shard_map/ppermute | solution.py:261
  124.4 5.6 %collective-permute-done.28.refs_26_ = bf16[128,1024]{1,0:T(8,128)(2,1)} collective-permute-done((bf16[128,1024]{1,0:T(8,128)(2,1)}, bf16[128,1024]{1,0:T(8,128)(2,1)}, u32[]{:S(2)}, u32[]{:S(2)}) %collective-permute-start.28) | collective-permute-done | bytes 262176 | tf_op jit(solution)/shard_map/ppermute | solution.py:261
  130.0 5.5 %collective-permute-done.22.refs_8_ = bf16[128,1024]{1,0:T(8,128)(2,1)S(1)} collective-permute-done((bf16[128,1024]{1,0:T(8,128)(2,1)}, bf16[128,1024]{1,0:T(8,128)(2,1)S(1)}, u32[]{:S(2)}, u32[]{:S(2)}) %collective-permute-start.22) | collective-permute-done | bytes 262176 | tf_op jit(solution)/shard_map/ppermute | solution.py:261
  136.3 3.2 %collective-permute-done.24.refs_10_ = bf16[128,1024]{1,0:T(8,128)(2,1)S(1)} collective-permute-done((bf16[128,1024]{1,0:T(8,128)(2,1)}, bf16[128,1024]{1,0:T(8,128)(2,1)S(1)}, u32[]{:S(2)}, u32[]{:S(2)}) %collective-permute-start.24) | collective-permute-done | bytes 262176 | tf_op jit(solution)/shard_map/ppermute | solution.py:261
  141.7 3.7 %shard_map.76 = (bf16[256,1024]{1,0:T(8,128)(2,1)}, bf16[256,1024]{1,0:T(8,128)(2,1)}, bf16[256,1024]{1,0:T(8,128)(2,1)}, bf16[256,1024]{1,0:T(8,128)(2,1)}) custom-call(s32[16]{0:T(128)S(1)} %copy-done.16, bf16[128,1024]{1,0:T(8,128)(2,1)S(1)} %get-tuple-element.103.refs_0_, bf16[128,1024]{1,0:T(8,128)(2,1)} %collective-permute-done.15.refs_1_, ...), custom_call_target="tpu_custom_call" | custom-call | bytes 4194304 | tf_op jit(solution)/shard_map/pallas_call | solution.py:150
  150.0 12.3 %shard_map.74 = (f32[1024,1024]{1,0:T(8,128)}, bf16[1024,1024]{1,0:T(8,128)(2,1)}, bf16[1024,1024]{1,0:T(8,128)(2,1)}) custom-call(s32[80]{0:T(128)} %reshape.20.a_table, s32[80]{0:T(128)} %reshape.21.b_table, bf16[1024,1024]{1,0:T(8,128)(2,1)} %c.1, bf16[8,2,5,128,128]{4,3,2,1,0:T(8,128)(2,1)} %a_blocks.1, bf16[8,2,5,128,128]{4,3,2,1,0:T(8,128)(2,1)} %b_blocks.1), custom_call_target="tpu_custom_call" | custom-call | flops 4294967296 | bytes 15728640 | tf_op jit(solution)/shard_map/pallas_call | solution.py:43
  162.3 8.5 %collective-permute-done.30.refs_1_ = bf16[256,1024]{1,0:T(8,128)(2,1)} collective-permute-done((bf16[256,1024]{1,0:T(8,128)(2,1)}, bf16[256,1024]{1,0:T(8,128)(2,1)}, u32[]{:S(2)}, u32[]{:S(2)}) %collective-permute-start.30) | collective-permute-done | bytes 524320 | tf_op jit(solution)/shard_map/ppermute | solution.py:270
  170.8 5.3 %shard_map.77.terms_ref = f32[1024,1024]{1,0:T(8,128)} custom-call(s32[5]{0:T(128)} %get-tuple-element.80.facts_ref, f32[1024,1024]{1,0:T(8,128)} %get-tuple-element.81.terms_ref, bf16[1024,1024]{1,0:T(8,128)(2,1)} %get-tuple-element.82.dense_ref, bf16[256,1024]{1,0:T(8,128)(2,1)} %get-tuple-element.95.refs_0_, ...), custom_call_target="tpu_custom_call", output_to_operand_aliasing={{}: (1, {})} | custom-call | flops 1073741824 | bytes 6291456 | tf_op jit(solution)/shard_map/pallas_call | solution.py:74
  177.8 5.3 %shard_map.78.terms_ref = f32[1024,1024]{1,0:T(8,128)} custom-call(s32[5]{0:T(128)} %get-tuple-element.80.facts_ref, f32[1024,1024]{1,0:T(8,128)} %shard_map.77.terms_ref, bf16[1024,1024]{1,0:T(8,128)(2,1)} %get-tuple-element.82.dense_ref, bf16[256,1024]{1,0:T(8,128)(2,1)} %copy-done.4, bf16[256,1024]{1,0:T(8,128)(2,1)} %copy-done.5), custom_call_target="tpu_custom_call", output_to_operand_aliasing={{}: (1, {})} | custom-call | flops 1073741824 | bytes 6291456 | tf_op jit(solution)/shard_map/pallas_call | solution.py:74
  184.4 6.1 %shard_map.80 = bf16[1024,1024]{1,0:T(8,128)(2,1)} custom-call(f32[1024,1024]{1,0:T(8,128)} %shard_map.78.terms_ref, bf16[1024,1024]{1,0:T(8,128)(2,1)} %get-tuple-element.99.dense_ref, bf16[1024,1024]{1,0:T(8,128)(2,1)} %bitcast.21), custom_call_target="tpu_custom_call" | custom-call | flops 2147483648 | bytes 10485760 | tf_op jit(solution)/shard_map/pallas_call | solution.py:102
  (74 shorter events, 17.3 us)
Async XLA Ops:
  65.4 117.7 %all-to-all-start.1 = ((bf16[16,64,1024]{2,1,0:T(8,128)(2,1)}), bf16[16,64,1024]{2,1,0:T(8,128)(2,1)S(1)}, u32[]{:S(2)}, u32[]{:S(2)}) async-start(bf16[16,64,1024]{2,1,0:T(8,128)(2,1)} %shard_map.79), calls=%async_computation.1 | async-start | bytes 4194304 | tf_op jit(solution)/shard_map/all_to_all | solution.py:265
  72.3 14.9 %collective-permute-start.8 = (bf16[128,1024]{1,0:T(8,128)(2,1)S(1)}, bf16[128,1024]{1,0:T(8,128)(2,1)S(1)}, u32[]{:S(2)}, u32[]{:S(2)}) collective-permute-start(bf16[128,1024]{1,0:T(8,128)(2,1)S(1)} %get-tuple-element.106), channel_id=1, source_target_pairs={{0,4},{4,8},{8,12},{12,0},{1,5},{5,9},{9,13},{13,1},{2,6},{6,10},{... | collective-permute-start | bytes 786440 | tf_op jit(solution)/shard_map/ppermute | solution.py:270
  73.7 13.5 %collective-permute-start.9 = (bf16[128,1024]{1,0:T(8,128)(2,1)S(1)}, bf16[128,1024]{1,0:T(8,128)(2,1)S(1)}, u32[]{:S(2)}, u32[]{:S(2)}) collective-permute-start(bf16[128,1024]{1,0:T(8,128)(2,1)S(1)} %get-tuple-element.105), channel_id=1, source_target_pairs={{0,8},{4,12},{8,0},{12,4},{1,9},{5,13},{9,1},{13,5},{2,10},{6,14},... | collective-permute-start | bytes 786440 | tf_op jit(solution)/shard_map/ppermute | solution.py:270
  74.3 15.0 %collective-permute-start.10 = (bf16[128,1024]{1,0:T(8,128)(2,1)S(1)}, bf16[128,1024]{1,0:T(8,128)(2,1)S(1)}, u32[]{:S(2)}, u32[]{:S(2)}) collective-permute-start(bf16[128,1024]{1,0:T(8,128)(2,1)S(1)} %get-tuple-element.104), channel_id=1, source_target_pairs={{0,12},{4,0},{8,4},{12,8},{1,13},{5,1},{9,5},{13,9},{2,14},{6,2},{... | collective-permute-start | bytes 786440 | tf_op jit(solution)/shard_map/ppermute | solution.py:270
  75.4 17.6 %collective-permute-start.15 = (bf16[128,1024]{1,0:T(8,128)(2,1)S(1)}, bf16[128,1024]{1,0:T(8,128)(2,1)}, u32[]{:S(2)}, u32[]{:S(2)}) collective-permute-start(bf16[128,1024]{1,0:T(8,128)(2,1)S(1)} %get-tuple-element.102), channel_id=1, source_target_pairs={{0,4},{4,8},{8,12},{12,0},{1,5},{5,9},{9,13},{13,1},{2,6},{6,10},{... | collective-permute-start | bytes 786440 | tf_op jit(solution)/shard_map/ppermute | solution.py:270
  76.5 19.9 %collective-permute-start.16 = (bf16[128,1024]{1,0:T(8,128)(2,1)S(1)}, bf16[128,1024]{1,0:T(8,128)(2,1)}, u32[]{:S(2)}, u32[]{:S(2)}) collective-permute-start(bf16[128,1024]{1,0:T(8,128)(2,1)S(1)} %get-tuple-element.101), channel_id=1, source_target_pairs={{0,8},{4,12},{8,0},{12,4},{1,9},{5,13},{9,1},{13,5},{2,10},{6,14},... | collective-permute-start | bytes 786440 | tf_op jit(solution)/shard_map/ppermute | solution.py:270
  87.2 11.0 %collective-permute-start.17 = (bf16[128,1024]{1,0:T(8,128)(2,1)S(1)}, bf16[128,1024]{1,0:T(8,128)(2,1)}, u32[]{:S(2)}, u32[]{:S(2)}) collective-permute-start(bf16[128,1024]{1,0:T(8,128)(2,1)S(1)} %get-tuple-element.100), channel_id=1, source_target_pairs={{0,12},{4,0},{8,4},{12,8},{1,13},{5,1},{9,5},{13,9},{2,14},{6,2},{... | collective-permute-start | bytes 786440 | tf_op jit(solution)/shard_map/ppermute | solution.py:270
  87.2 11.0 %collective-permute-start.11 = (bf16[128,1024]{1,0:T(8,128)(2,1)S(1)}, bf16[128,1024]{1,0:T(8,128)(2,1)S(1)}, u32[]{:S(2)}, u32[]{:S(2)}) collective-permute-start(bf16[128,1024]{1,0:T(8,128)(2,1)S(1)} %get-tuple-element.107.refs_0_.refs_16_), channel_id=1, source_target_pairs={{0,1},{1,0},{2,3},{3,2},{4,5},{5,4},{6,7},{7,6},{8,9},{9,8},{10,11... | collective-permute-start | bytes 786440 | tf_op jit(solution)/shard_map/ppermute | solution.py:261
  89.3 9.5 %collective-permute-start.12 = (bf16[128,1024]{1,0:T(8,128)(2,1)S(1)}, bf16[128,1024]{1,0:T(8,128)(2,1)S(1)}, u32[]{:S(2)}, u32[]{:S(2)}) collective-permute-start(bf16[128,1024]{1,0:T(8,128)(2,1)S(1)} %collective-permute-done.8.refs_1_.refs_17_), channel_id=1, source_target_pairs={{0,1},{1,0},{2,3},{3,2},{4,5},{5,4},{6,7},{7,6},{8,9},{9,8},{10,11... | collective-permute-start | bytes 786440 | tf_op jit(solution)/shard_map/ppermute | solution.py:261
  92.9 5.9 %collective-permute-start.13 = (bf16[128,1024]{1,0:T(8,128)(2,1)S(1)}, bf16[128,1024]{1,0:T(8,128)(2,1)S(1)}, u32[]{:S(2)}, u32[]{:S(2)}) collective-permute-start(bf16[128,1024]{1,0:T(8,128)(2,1)S(1)} %collective-permute-done.9.refs_2_.refs_18_), channel_id=1, source_target_pairs={{0,1},{1,0},{2,3},{3,2},{4,5},{5,4},{6,7},{7,6},{8,9},{9,8},{10,11... | collective-permute-start | bytes 786440 | tf_op jit(solution)/shard_map/ppermute | solution.py:261
  98.2 6.7 %collective-permute-start.18 = (bf16[128,1024]{1,0:T(8,128)(2,1)S(1)}, bf16[128,1024]{1,0:T(8,128)(2,1)}, u32[]{:S(2)}, u32[]{:S(2)}) collective-permute-start(bf16[128,1024]{1,0:T(8,128)(2,1)S(1)} %get-tuple-element.103.refs_0_), channel_id=1, source_target_pairs={{0,1},{1,0},{2,3},{3,2},{4,5},{5,4},{6,7},{7,6},{8,9},{9,8},{10,11... | collective-permute-start | bytes 786440 | tf_op jit(solution)/shard_map/ppermute | solution.py:261
  98.2 6.7 %collective-permute-start.19 = (bf16[128,1024]{1,0:T(8,128)(2,1)}, bf16[128,1024]{1,0:T(8,128)(2,1)}, u32[]{:S(2)}, u32[]{:S(2)}) collective-permute-start(bf16[128,1024]{1,0:T(8,128)(2,1)} %collective-permute-done.15.refs_1_), channel_id=1, source_target_pairs={{0,1},{1,0},{2,3},{3,2},{4,5},{5,4},{6,7},{7,6},{8,9},{9,8},{10,11... | collective-permute-start | bytes 786440 | tf_op jit(solution)/shard_map/ppermute | solution.py:261
  98.7 6.2 %collective-permute-start.20 = (bf16[128,1024]{1,0:T(8,128)(2,1)}, bf16[128,1024]{1,0:T(8,128)(2,1)}, u32[]{:S(2)}, u32[]{:S(2)}) collective-permute-start(bf16[128,1024]{1,0:T(8,128)(2,1)} %collective-permute-done.16.refs_2_), channel_id=1, source_target_pairs={{0,1},{1,0},{2,3},{3,2},{4,5},{5,4},{6,7},{7,6},{8,9},{9,8},{10,11... | collective-permute-start | bytes 786440 | tf_op jit(solution)/shard_map/ppermute | solution.py:261
  98.9 6.0 %collective-permute-start.21 = (bf16[128,1024]{1,0:T(8,128)(2,1)}, bf16[128,1024]{1,0:T(8,128)(2,1)}, u32[]{:S(2)}, u32[]{:S(2)}) collective-permute-start(bf16[128,1024]{1,0:T(8,128)(2,1)} %collective-permute-done.17.refs_3_), channel_id=1, source_target_pairs={{0,1},{1,0},{2,3},{3,2},{4,5},{5,4},{6,7},{7,6},{8,9},{9,8},{10,11... | collective-permute-start | bytes 786440 | tf_op jit(solution)/shard_map/ppermute | solution.py:261
  103.2 21.2 %collective-permute-start.26 = (bf16[128,1024]{1,0:T(8,128)(2,1)}, bf16[128,1024]{1,0:T(8,128)(2,1)}, u32[]{:S(2)}, u32[]{:S(2)}) collective-permute-start(bf16[128,1024]{1,0:T(8,128)(2,1)} %get-tuple-element.89), channel_id=1, source_target_pairs={{0,2},{2,0},{1,3},{3,1},{4,6},{6,4},{5,7},{7,5},{8,10},{10,8},{9,1... | collective-permute-start | bytes 786440 | tf_op jit(solution)/shard_map/ppermute | solution.py:261
  105.2 24.9 %collective-permute-start.28 = (bf16[128,1024]{1,0:T(8,128)(2,1)}, bf16[128,1024]{1,0:T(8,128)(2,1)}, u32[]{:S(2)}, u32[]{:S(2)}) collective-permute-start(bf16[128,1024]{1,0:T(8,128)(2,1)} %get-tuple-element.90), channel_id=1, source_target_pairs={{0,2},{2,0},{1,3},{3,1},{4,6},{6,4},{5,7},{7,5},{8,10},{10,8},{9,1... | collective-permute-start | bytes 786440 | tf_op jit(solution)/shard_map/ppermute | solution.py:261
  108.7 26.9 %collective-permute-start.22 = (bf16[128,1024]{1,0:T(8,128)(2,1)}, bf16[128,1024]{1,0:T(8,128)(2,1)S(1)}, u32[]{:S(2)}, u32[]{:S(2)}) collective-permute-start(bf16[128,1024]{1,0:T(8,128)(2,1)} %get-tuple-element.83), channel_id=1, source_target_pairs={{0,2},{2,0},{1,3},{3,1},{4,6},{6,4},{5,7},{7,5},{8,10},{10,8},{9,1... | collective-permute-start | bytes 786440 | tf_op jit(solution)/shard_map/ppermute | solution.py:261
  110.3 29.2 %collective-permute-start.24 = (bf16[128,1024]{1,0:T(8,128)(2,1)}, bf16[128,1024]{1,0:T(8,128)(2,1)S(1)}, u32[]{:S(2)}, u32[]{:S(2)}) collective-permute-start(bf16[128,1024]{1,0:T(8,128)(2,1)} %get-tuple-element.84), channel_id=1, source_target_pairs={{0,2},{2,0},{1,3},{3,1},{4,6},{6,4},{5,7},{7,5},{8,10},{10,8},{9,1... | collective-permute-start | bytes 786440 | tf_op jit(solution)/shard_map/ppermute | solution.py:261
  124.4 15.1 %collective-permute-start.27 = (bf16[128,1024]{1,0:T(8,128)(2,1)}, bf16[128,1024]{1,0:T(8,128)(2,1)S(1)}, u32[]{:S(2)}, u32[]{:S(2)}) collective-permute-start(bf16[128,1024]{1,0:T(8,128)(2,1)} %collective-permute-done.26.refs_24_), channel_id=1, source_target_pairs={{0,1},{1,0},{2,3},{3,2},{4,5},{5,4},{6,7},{7,6},{8,9},{9,8},{10,11... | collective-permute-start | bytes 786440 | tf_op jit(solution)/shard_map/ppermute | solution.py:261
  130.0 9.5 %collective-permute-start.29 = (bf16[128,1024]{1,0:T(8,128)(2,1)}, bf16[128,1024]{1,0:T(8,128)(2,1)S(1)}, u32[]{:S(2)}, u32[]{:S(2)}) collective-permute-start(bf16[128,1024]{1,0:T(8,128)(2,1)} %collective-permute-done.28.refs_26_), channel_id=1, source_target_pairs={{0,1},{1,0},{2,3},{3,2},{4,5},{5,4},{6,7},{7,6},{8,9},{9,8},{10,11... | collective-permute-start | bytes 786440 | tf_op jit(solution)/shard_map/ppermute | solution.py:261
  136.3 3.3 %collective-permute-start.23 = (bf16[128,1024]{1,0:T(8,128)(2,1)S(1)}, bf16[128,1024]{1,0:T(8,128)(2,1)S(1)}, u32[]{:S(2)}, u32[]{:S(2)}) collective-permute-start(bf16[128,1024]{1,0:T(8,128)(2,1)S(1)} %collective-permute-done.22.refs_8_), channel_id=1, source_target_pairs={{0,1},{1,0},{2,3},{3,2},{4,5},{5,4},{6,7},{7,6},{8,9},{9,8},{10,11... | collective-permute-start | bytes 786440 | tf_op jit(solution)/shard_map/ppermute | solution.py:261
  145.5 25.4 %collective-permute-start.30 = (bf16[256,1024]{1,0:T(8,128)(2,1)}, bf16[256,1024]{1,0:T(8,128)(2,1)}, u32[]{:S(2)}, u32[]{:S(2)}) collective-permute-start(bf16[256,1024]{1,0:T(8,128)(2,1)} %get-tuple-element.96), channel_id=1, source_target_pairs={{0,4},{4,8},{8,12},{12,0},{1,5},{5,9},{9,13},{13,1},{2,6},{6,10},{... | collective-permute-start | bytes 1572872 | tf_op jit(solution)/shard_map/ppermute | solution.py:270
  146.8 29.4 %collective-permute-start.31 = (bf16[256,1024]{1,0:T(8,128)(2,1)}, bf16[256,1024]{1,0:T(8,128)(2,1)S(1)}, u32[]{:S(2)}, u32[]{:S(2)}) collective-permute-start(bf16[256,1024]{1,0:T(8,128)(2,1)} %get-tuple-element.97), channel_id=1, source_target_pairs={{0,8},{4,12},{8,0},{12,4},{1,9},{5,13},{9,1},{13,5},{2,10},{6,14},... | collective-permute-start | bytes 1572872 | tf_op jit(solution)/shard_map/ppermute | solution.py:270
  147.5 28.6 %collective-permute-start.32 = (bf16[256,1024]{1,0:T(8,128)(2,1)}, bf16[256,1024]{1,0:T(8,128)(2,1)S(1)}, u32[]{:S(2)}, u32[]{:S(2)}) collective-permute-start(bf16[256,1024]{1,0:T(8,128)(2,1)} %get-tuple-element.98), channel_id=1, source_target_pairs={{0,12},{4,0},{8,4},{12,8},{1,13},{5,1},{9,5},{13,9},{2,14},{6,2},{... | collective-permute-start | bytes 1572872 | tf_op jit(solution)/shard_map/ppermute | solution.py:270
  (17 other events, 59.0 us)
